TPU v7x, 256 devices: a whole 4x4x8 slice. The times are simulated.
256 devices in a mesh: gx: 4 (over z_hi), gy: 8 (over x, core), gz: 8 (over y, z_lo).
Axes of the slice: x: 4, y: 4, z: 8 (z_hi: 4, z_lo: 2; z = z_hi * 2 + z_lo), core: 2. Of those that a mesh axis runs over, the one named last changes fastest.
Arguments:
- schur: float32 [4, 8, 8, 1536, 1536], P('gx', 'gy', 'gz'), as said below
- start_block: float32 [4, 8, 8, 6, 256, 32], P('gx', 'gy', 'gz'), may hold values from -6 to 6
- resid: float32 [4, 8, 8, 1536, 128], P('gx', 'gy', 'gz'), may hold values from -6 to 6
- group_of: int32 [64], replicated, may hold values from 0 to 15, as said below
Outputs:
- correction: float32 [4, 8, 8, 1536, 128], P('gx', 'gy', 'gz')
Inputs may be any that keep to these rules, and one draw needn't show every extreme that they name: Each subdomain's schur is symmetric positive definite. `group_of`: each of the 16 groups has exactly 4 subdomains.
All inputs are finite; a program needn't handle non-finite values.
Results may differ from a plain program's by a relative error of at most 0.00022.
Values sent between devices are 32-bit elements; how exact they have to be, the bound alone decides.
A program may use at most 128 MiB of HBM per device.

v0:
```python
import jax
import jax.numpy as jnp
from jax import lax
from jax.sharding import Mesh
from jax.sharding import PartitionSpec as P

NS_ITERS = 3
SUB_ITERS = 2
GROUP_SIZE = 4
GY = ("gy_0", "gy_1")
GZ = ("gz_0", "gz_1")


precise = lax.Precision.HIGHEST


def extended(block, sides, width):
    for axis, dim in sides:
        count = lax.axis_size(axis)
        forward = [(i, i + 1) for i in range(count - 1)]
        forward.append((count - 1, 0))
        backward = [(target, source) for source, target in forward]
        low = lax.ppermute(
            lax.slice_in_dim(block, block.shape[dim] - width, None, axis=dim), axis, forward
        )
        high = lax.ppermute(lax.slice_in_dim(block, 0, width, axis=dim), axis, backward)
        block = jnp.concatenate([low, block, high], axis=dim)
    return block


def in_blocks(shard, dim, devices):
    shape = shard.shape
    tiles = shard.reshape(*shape[:dim], devices, shape[dim] // devices, *shape[dim + 1 :])
    return jnp.moveaxis(tiles, dim, 0)


def sum_at_owner(shard, axis, dim):
    devices = lax.axis_size(axis)
    tiles = lax.all_to_all(in_blocks(shard, dim, devices), axis, 0, 0, tiled=True)
    return jnp.sum(tiles, axis=0)


def summed_rows(shard, axes, dim):
    far, near = axes
    tiles = in_blocks(shard, dim, lax.axis_size(far))
    nearer = sum_at_owner(tiles, near, dim + 1)
    arrived = lax.all_to_all(nearer, far, split_axis=0, concat_axis=0, tiled=True)
    return arrived.sum(axis=0)


def padded_to(lines, devices):
    spare = -lines.shape[0] % devices
    if not spare:
        return lines
    return jnp.concatenate([lines, jnp.zeros((spare, *lines.shape[1:]), lines.dtype)])


def copy_for_each(shard, axis):
    copies = jnp.broadcast_to(shard, (lax.axis_size(axis), *shard.shape))
    return lax.all_to_all(copies, axis, split_axis=0, concat_axis=0, tiled=True)


def joined_along(tiles, dim):
    shape = list(tiles.shape[1:])
    shape[dim] *= tiles.shape[0]
    return jnp.moveaxis(tiles, 0, dim).reshape(shape)


def whole_of(shard, axes, dim):
    far, near = axes
    leading = copy_for_each(shard, far)
    tiles = jnp.swapaxes(copy_for_each(leading, near), 0, 1)
    return joined_along(tiles.reshape(-1, *shard.shape), dim)


def total_of(shard, axes):
    lines = shard.reshape(-1, shard.shape[-1])
    own = summed_rows(padded_to(lines, lax.axis_size(axes[0]) * lax.axis_size(axes[1])), axes, 0)
    whole = whole_of(own, axes, 0)
    return whole[: len(lines)].reshape(shard.shape)


def swap_faces(stack):
    along_x = extended(stack[0:2], (("gx", 0),), 1)
    along_y = extended(stack[2:4], ((GY, 0),), 1)
    along_z = extended(stack[4:6], ((GZ, 0),), 1)
    return jnp.stack([along_x[0], along_x[3], along_y[0], along_y[3], along_z[0], along_z[3]])


def newton_inverse(matrices):
    diag_vals = jnp.diagonal(matrices, axis1=1, axis2=2)
    identity = jnp.eye(matrices.shape[1], dtype=jnp.float32)
    inverse = identity[None] / diag_vals[:, None, :]
    for sweep in range(NS_ITERS):
        product = jnp.einsum("fij,fjk->fik", matrices, inverse, precision=precise)
        inverse = 2.0 * inverse - jnp.einsum("fij,fjk->fik", inverse, product, precision=precise)
    return inverse


def right_factor(factor, image):
    return jax.scipy.linalg.solve_triangular(factor, image.T, lower=True).T


def subspace(own, partner, inverse, starts):
    basis = starts
    for sweep in range(SUB_ITERS):
        image = jnp.einsum("fij,fjc->fic", partner, basis, precision=precise)
        image = jnp.einsum("fij,fjc->fic", inverse, image, precision=precise)
        image = jnp.einsum("fij,fjc->fic", own, image, precision=precise)
        gram = jnp.einsum("fic,fid->fcd", image, image, precision=precise)
        factor = jnp.linalg.cholesky(gram)
        basis = jax.vmap(right_factor)(factor, image)
    return basis


def solve_one(matrix, rhs):
    factor = jnp.linalg.cholesky(matrix)
    return jax.scipy.linalg.cho_solve((factor, True), rhs)


def per_device(schur, start_block, resid, group_of):
    matrix_full = schur[0, 0, 0]
    order = matrix_full.shape[0]
    width = order // 6
    starts = start_block[0, 0, 0]
    ncon = starts.shape[2]
    coarse_n = 6 * ncon
    resid_one = resid[0, 0, 0]
    columns = resid_one.shape[1]
    own = jnp.stack(
        [matrix_full[f * width : (f + 1) * width, f * width : (f + 1) * width] for f in range(6)]
    )
    partner = swap_faces(own)
    inverse = newton_inverse(own + partner)
    basis = subspace(own, partner, inverse, starts)
    rows_grouped = matrix_full.reshape(order, 6, width)
    side = jnp.einsum("igj,gjc->igc", rows_grouped, basis, precision=precise).reshape(
        6, width, 6, ncon
    )
    coarse_local = jnp.einsum("fic,figd->fcgd", basis, side, precision=precise).reshape(
        coarse_n, coarse_n
    )
    rhs_local = jnp.einsum(
        "fic,fin->fcn", basis, resid_one.reshape(6, width, columns), precision=precise
    ).reshape(coarse_n, columns)
    linear = lax.axis_index(GY) * lax.axis_size(GZ) + lax.axis_index(GZ)
    plane = group_of.shape[0]
    groups = plane // GROUP_SIZE
    my_group = group_of[linear]
    picked = (jnp.arange(groups, dtype=jnp.int32) == my_group).astype(jnp.float32)
    total_matrix, total_rhs = (
        total_of(picked[:, None, None] * coarse_local[None], (("gy_0", "gy_1", "gz_0"), "gz_1")),
        total_of(picked[:, None, None] * rhs_local[None], (("gy_0", "gy_1", "gz_0"), "gz_1")),
    )
    matrix = jnp.einsum("g,gab->ab", picked, total_matrix, precision=precise)
    rhs = jnp.einsum("g,gab->ab", picked, total_rhs, precision=precise)
    answer = solve_one(matrix, rhs)
    w_faces = jnp.einsum("fic,fcn->fin", basis, answer.reshape(6, ncon, columns), precision=precise)
    products = jnp.einsum("fij,fjn->fin", own, w_faces, precision=precise)
    partner_y = swap_faces(products)
    correction = jnp.einsum("fij,fjn->fin", inverse, products + partner_y, precision=precise)
    return correction.reshape(order, columns)[None, None, None]


def solution(mesh):
    split = Mesh(
        mesh.devices.reshape(mesh.shape["gx"], 4, 2, 4, 2), ("gx", "gy_0", "gy_1", "gz_0", "gz_1")
    )
    in_specs = (
        P("gx", GY, GZ, None, None),
        P("gx", GY, GZ, None, None, None),
        P("gx", GY, GZ, None, None),
        P(),
    )
    out_specs = P("gx", GY, GZ, None, None)
    return jax.shard_map(
        per_device, mesh=split, in_specs=in_specs, out_specs=out_specs, check_vma=False
    )
```

profile of v0, /device:TPU:1, one launch (start us, length us, event | category | flops | bytes accessed | tf_op | source)
XLA Modules:
  0.0 454.1 jit_solution(18231639689756088349)
XLA Ops:
  0.0 2.3 slice_bitcast_fusion.1
  2.3 3.8 collective-permute-start
  6.1 3.0 collective-permute-start.1
  9.2 2.1 collective-permute-start.2
  20.0 4.5 collective-permute-start.5
  28.4 1.8 collective-permute-done.4
  31.1 2.1 collective-permute-done.5
  34.4 1.3 add.59
  35.7 17.6 %copy.51 = f32[6,256,256]{0,2,1:T(8,128)} copy(f32[6,256,256]{2,1,0:T(8,128)} %add.59) | data formatting | bytes 3145728 | tf_op jit(solution)/shard_map/add | solution.py:134
  53.3 2.3 gather_fusion
  55.7 3.1 fusion.4
  58.8 1.8 multiply_subtract_fusion.2
  60.7 1.7 fusion.46
  62.3 1.8 multiply_subtract_fusion.1
  64.1 1.7 fusion.47
  65.8 1.8 multiply_subtract_fusion
  67.6 1.7 fusion.23
  69.3 1.5 fusion.48
  70.9 1.5 fusion.49
  72.9 17.6 %custom-call.30 = f32[6,32,32]{2,1,0:T(8,128)S(1)} custom-call(f32[6,32,32]{2,1,0:T(8,128)S(1)} %fusion.28), custom_call_target="Cholesky" | custom-call | tf_op jit(solution)/shard_map/jit(cholesky)/cholesky | solution.py:111
  90.7 14.8 %custom-call.31 = f32[6,1,32,32]{2,3,1,0:T(8,128)S(1)} custom-call(f32[6,1,32,32]{3,2,1,0:T(8,128)S(1)} %select_bitcast_fusion.1), custom_call_target="InvertDiagBlocksLowerTriangular" | custom-call | tf_op jit(solution)/shard_map/vmap(jit(_solve_triangular))/triangular_solve | solution.py:101
  105.9 3.0 fusion.51
  109.0 1.5 fusion.52
  110.5 1.5 fusion.53
  112.5 17.6 %custom-call.32 = f32[6,32,32]{2,1,0:T(8,128)S(1)} custom-call(f32[6,32,32]{2,1,0:T(8,128)S(1)} %fusion.26), custom_call_target="Cholesky" | custom-call | tf_op jit(solution)/shard_map/jit(cholesky)/cholesky | solution.py:111
  130.3 14.8 %custom-call.33 = f32[6,1,32,32]{2,3,1,0:T(8,128)S(1)} custom-call(f32[6,1,32,32]{3,2,1,0:T(8,128)S(1)} %select_bitcast_fusion), custom_call_target="InvertDiagBlocksLowerTriangular" | custom-call | tf_op jit(solution)/shard_map/vmap(jit(_solve_triangular))/triangular_solve | solution.py:101
  146.4 1.3 copy.64
  147.7 4.6 %all-to-all-start.4 = ((f32[2,32,48,128]{3,2,1,0:T(8,128)}), f32[2,32,48,128]{3,2,1,0:T(8,128)}, u32[]{:S(2)}, u32[]{:S(2)}) async-start(f32[2,32,48,128]{3,2,1,0:T(8,128)} %copy.64), calls=%async_computation.4 | async-start | bytes 3145728 | tf_op jit(solution)/shard_map/all_to_all | solution.py:39
  152.3 10.0 %copy.57 = f32[1,1,1,1536,1536]{3,4,2,1,0:T(8,128)} copy(f32[1,1,1,1536,1536]{4,3,2,1,0:T(8,128)} %param.7) | data formatting | bytes 18874368 | tf_op args[0]
  162.3 7.9 %fusion.55 = f32[6,32,1536]{2,1,0:T(8,128)S(1)} fusion(f32[6,32,256]{2,1,0:T(8,128)S(1)} %fusion.19, f32[1536,6,256]{0,2,1:T(8,128)} %bitcast.159), kind=kOutput, calls=%fused_computation.123 | convolution fusion | flops 905969664 | bytes 10813440 | tf_op jit(solution)/shard_map/igj,gjc->igc/dot_general | solution.py:137
  170.2 2.8 fusion.7
  174.3 1.9 copy.61
  176.2 5.2 %all-to-all-start = ((f32[2,32,48,192]{3,2,1,0:T(8,128)}), f32[2,32,48,192]{3,2,1,0:T(8,128)}, u32[]{:S(2)}, u32[]{:S(2)}) async-start(f32[2,32,48,192]{3,2,1,0:T(8,128)} %copy.61), calls=%async_computation | async-start | bytes 6291456 | tf_op jit(solution)/shard_map/all_to_all | solution.py:39
  181.4 2.5 reduce_sum.38
  183.9 32.8 %all-to-all-done = f32[2,32,48,192]{3,2,1,0:T(8,128)} async-done(((f32[2,32,48,192]{3,2,1,0:T(8,128)}), f32[2,32,48,192]{3,2,1,0:T(8,128)}, u32[]{:S(2)}, u32[]{:S(2)}) %all-to-all-start) | async-done | bytes 2359328 | tf_op jit(solution)/shard_map/all_to_all | solution.py:39
  216.7 8.9 %all-to-all-start.5 = ((f32[32,48,128]{2,1,0:T(8,128)}), f32[32,48,128]{2,1,0:T(8,128)S(1)}, u32[]{:S(2)}, u32[]{:S(2)}) async-start(f32[32,48,128]{2,1,0:T(8,128)} %reduce_sum.38), calls=%async_computation.5 | async-start | bytes 1572864 | tf_op jit(solution)/shard_map/all_to_all | solution.py:47
  225.6 3.5 reduce_sum.36
  229.1 10.0 %all-to-all-done.5 = f32[32,48,128]{2,1,0:T(8,128)S(1)} async-done(((f32[32,48,128]{2,1,0:T(8,128)}), f32[32,48,128]{2,1,0:T(8,128)S(1)}, u32[]{:S(2)}, u32[]{:S(2)}) %all-to-all-start.5) | async-done | bytes 786464 | tf_op jit(solution)/shard_map/all_to_all | solution.py:47
  239.1 5.4 %all-to-all-start.1 = ((f32[32,48,192]{2,1,0:T(8,128)}), f32[32,48,192]{2,1,0:T(8,128)}, u32[]{:S(2)}, u32[]{:S(2)}) async-start(f32[32,48,192]{2,1,0:T(8,128)} %reduce_sum.36), calls=%async_computation.1 | async-start | bytes 3145728 | tf_op jit(solution)/shard_map/all_to_all | solution.py:47
  244.6 21.4 %all-to-all-done.1 = f32[32,48,192]{2,1,0:T(8,128)} async-done(((f32[32,48,192]{2,1,0:T(8,128)}), f32[32,48,192]{2,1,0:T(8,128)}, u32[]{:S(2)}, u32[]{:S(2)}) %all-to-all-start.1) | async-done | bytes 1179680 | tf_op jit(solution)/shard_map/all_to_all | solution.py:47
  267.0 5.3 %all-to-all-start.6 = ((f32[32,48,128]{2,1,0:T(8,128)}), f32[32,48,128]{2,1,0:T(8,128)S(1)}, u32[]{:S(2)}, u32[]{:S(2)}) async-start(f32[32,48,128]{2,1,0:T(8,128)} %broadcast_in_dim.28), calls=%async_computation.6 | async-start | bytes 1572864 | tf_op jit(solution)/shard_map/all_to_all | solution.py:60
  272.3 1.5 reduce_sum.37
  273.8 12.0 %all-to-all-done.6 = f32[32,48,128]{2,1,0:T(8,128)S(1)} async-done(((f32[32,48,128]{2,1,0:T(8,128)}), f32[32,48,128]{2,1,0:T(8,128)S(1)}, u32[]{:S(2)}, u32[]{:S(2)}) %all-to-all-start.6) | async-done | bytes 786464 | tf_op jit(solution)/shard_map/all_to_all | solution.py:60
  286.0 26.8 %all_to_all.40 = f32[32,48,192]{2,1,0:T(8,128)S(1)} all-to-all(f32[32,48,192]{2,1,0:T(8,128)S(1)} %broadcast_in_dim.26), channel_id=1, replica_groups=mesh['gx'=4,'gy_0'=4,'gy_1'=2,'gz_0'=4,'gz_1'=2] {'gy_0','gy_1','gz_0'}, dimensions={0} | all-to-all | bytes 2359296 | tf_op jit(solution)/shard_map/all_to_all | solution.py:60
  312.9 21.7 %all_to_all.41 = f32[2,32,48,128]{3,2,1,0:T(8,128)} all-to-all(f32[2,32,48,128]{3,2,1,0:T(8,128)S(1)} %broadcast_in_dim.29), channel_id=1, replica_groups=mesh['gx'=4,'gy_0'=4,'gy_1'=2,'gz_0'=4,'gz_1'=2] {'gz_1'}, dimensions={0} | all-to-all | bytes 3145728 | tf_op jit(solution)/shard_map/all_to_all | solution.py:60
  334.5 2.1 broadcast_in_dim.27
  336.6 5.4 %all-to-all-start.3 = ((f32[2,32,48,192]{3,2,1,0:T(8,128)}), f32[2,32,48,192]{3,2,1,0:T(8,128)}, u32[]{:S(2)}, u32[]{:S(2)}) async-start(f32[2,32,48,192]{3,2,1,0:T(8,128)} %broadcast_in_dim.27), calls=%async_computation.3 | async-start | bytes 6291456 | tf_op jit(solution)/shard_map/all_to_all | solution.py:60
  342.0 1.6 copy.65
  343.6 2.2 fusion.2
  345.8 30.6 %all-to-all-done.3 = f32[2,32,48,192]{3,2,1,0:T(8,128)} async-done(((f32[2,32,48,192]{3,2,1,0:T(8,128)}), f32[2,32,48,192]{3,2,1,0:T(8,128)}, u32[]{:S(2)}, u32[]{:S(2)}) %all-to-all-start.3) | async-done | bytes 2359328 | tf_op jit(solution)/shard_map/all_to_all | solution.py:60
  376.4 2.2 copy.62
  378.6 3.6 fusion
  382.4 11.7 %cholesky.79 = f32[128,128]{1,0:T(8,128)S(1)} custom-call(f32[128,128]{1,0:T(8,128)S(1)} %cholesky.189), custom_call_target="Cholesky" | custom-call | tf_op jit(solution)/shard_map/jit(cholesky)/cholesky | solution.py:117
  394.2 9.8 %custom-call.24 = f32[1,128,128]{1,2,0:T(8,128)S(1)} custom-call(f32[1,128,128]{2,1,0:T(8,128)S(1)} %get-tuple-element.40), custom_call_target="InvertDiagBlocksLowerTriangular" | custom-call | tf_op jit(solution)/shard_map/jit(cholesky)/cholesky | solution.py:117
  404.4 6.0 %cholesky.138 = f32[64,64]{1,0:T(8,128)S(1)} custom-call(f32[64,64]{1,0:T(8,128)S(1)} %convolution_subtract_fusion.2), custom_call_target="Cholesky" | custom-call | tf_op jit(solution)/shard_map/jit(cholesky)/cholesky | solution.py:117
  413.1 19.7 %custom-call.25 = f32[2,128,128]{1,2,0:T(8,128)S(1)} custom-call(f32[2,128,128]{2,1,0:T(8,128)S(1)} %pad_maximum_fusion), custom_call_target="InvertDiagBlocksLowerTriangular" | custom-call | tf_op jit(solution)/shard_map/jit(_cho_solve)/triangular_solve | solution.py:118
  434.2 1.5 fusion.57
  435.7 1.5 fusion.58
  437.3 1.2 collective-permute-start.6
  438.5 2.5 collective-permute-start.7
  440.9 4.3 collective-permute-start.8
  445.2 3.5 collective-permute-start.11
  449.6 1.8 collective-permute-done.10
  451.4 2.4 fusion.10
  (112 shorter events, 24.6 us)
Async XLA Ops:
  0.0 145.5 %copy-start = (f32[1,1,1,1536,128]{4,3,2,1,0:T(8,128)S(1)}, f32[1,1,1,1536,128]{4,3,2,1,0:T(8,128)}, u32[]{:S(2)}) copy-start(f32[1,1,1,1536,128]{4,3,2,1,0:T(8,128)} %param.9) | copy-start | bytes 2359300
  2.3 17.7 %collective-permute-start = (f32[1,256,256]{2,1,0:T(8,128)}, f32[1,256,256]{2,1,0:T(8,128)}, u32[]{:S(2)}, u32[]{:S(2)}) collective-permute-start(f32[1,256,256]{2,1,0:T(8,128)} %get-tuple-element.31), channel_id=1, source_target_pairs={{0,64},{64,128},{128,192},{192,0},{1,65},{65,129},{129,193},{193,1... | collective-permute-start | bytes 786440 | tf_op jit(solution)/shard_map/ppermute | solution.py:23
  6.1 19.4 %collective-permute-start.1 = (f32[1,256,256]{2,1,0:T(8,128)}, f32[1,256,256]{2,1,0:T(8,128)}, u32[]{:S(2)}, u32[]{:S(2)}) collective-permute-start(f32[1,256,256]{2,1,0:T(8,128)} %get-tuple-element.32), channel_id=1, source_target_pairs={{64,0},{128,64},{192,128},{0,192},{65,1},{129,65},{193,129},{1,193... | collective-permute-start | bytes 786440 | tf_op jit(solution)/shard_map/ppermute | solution.py:26
  9.2 17.3 %collective-permute-start.2 = (f32[1,256,256]{2,1,0:T(8,128)S(1)}, f32[1,256,256]{2,1,0:T(8,128)}, u32[]{:S(2)}, u32[]{:S(2)}) collective-permute-start(f32[1,256,256]{2,1,0:T(8,128)S(1)} %get-tuple-element.29), channel_id=1, source_target_pairs={{0,8},{8,16},{16,24},{24,32},{32,40},{40,48},{48,56},{56,0},{1,9},... | collective-permute-start | bytes 786440 | tf_op jit(solution)/shard_map/ppermute | solution.py:23
  11.2 16.2 %collective-permute-start.3 = (f32[1,256,256]{2,1,0:T(8,128)S(1)}, f32[1,256,256]{2,1,0:T(8,128)}, u32[]{:S(2)}, u32[]{:S(2)}) collective-permute-start(f32[1,256,256]{2,1,0:T(8,128)S(1)} %get-tuple-element.30), channel_id=1, source_target_pairs={{8,0},{16,8},{24,16},{32,24},{40,32},{48,40},{56,48},{0,56},{9,1},... | collective-permute-start | bytes 786440 | tf_op jit(solution)/shard_map/ppermute | solution.py:26
  11.2 19.0 %collective-permute-start.4 = (f32[1,256,256]{2,1,0:T(8,128)S(1)}, f32[1,256,256]{2,1,0:T(8,128)}, u32[]{:S(2)}, u32[]{:S(2)}) collective-permute-start(f32[1,256,256]{2,1,0:T(8,128)S(1)} %get-tuple-element.28), channel_id=1, source_target_pairs={{0,1},{1,2},{2,3},{3,4},{4,5},{5,6},{6,7},{7,0},{8,9},{9,10},{10,1... | collective-permute-start | bytes 786440 | tf_op jit(solution)/shard_map/ppermute | solution.py:23
  12.9 5.7 %copy-start.10 = (s32[64]{0:T(128)S(1)}, s32[64]{0:T(128)}, u32[]{:S(2)}) copy-start(s32[64]{0:T(128)} %param.10) | copy-start | bytes 772
  20.0 13.2 %collective-permute-start.5 = (f32[1,256,256]{2,1,0:T(8,128)S(1)}, f32[1,256,256]{2,1,0:T(8,128)S(1)}, u32[]{:S(2)}, u32[]{:S(2)}) collective-permute-start(f32[1,256,256]{2,1,0:T(8,128)S(1)} %get-tuple-element.27), channel_id=1, source_target_pairs={{1,0},{2,1},{3,2},{4,3},{5,4},{6,5},{7,6},{0,7},{9,8},{10,9},{11,1... | collective-permute-start | bytes 786440 | tf_op jit(solution)/shard_map/ppermute | solution.py:26
  33.3 1.1 copy-start.6
  35.7 20.0 %copy-start.8 = (f32[256,256]{1,0:T(8,128)S(1)}, f32[256,256]{1,0:T(8,128)}, u32[]{:S(2)}) copy-start(f32[256,256]{1,0:T(8,128)} %fusion.16) | copy-start | bytes 786436
  58.8 1.9 copy-start.2
  65.8 1.8 copy-start.7
  65.8 1.8 copy-start.9
  67.6 3.3 copy-start.3
  105.5 3.5 copy-start.4
  147.7 28.5 %all-to-all-start.4 = ((f32[2,32,48,128]{3,2,1,0:T(8,128)}), f32[2,32,48,128]{3,2,1,0:T(8,128)}, u32[]{:S(2)}, u32[]{:S(2)}) async-start(f32[2,32,48,128]{3,2,1,0:T(8,128)} %copy.64), calls=%async_computation.4 | async-start | bytes 3145728 | tf_op jit(solution)/shard_map/all_to_all | solution.py:39
  176.2 40.5 %all-to-all-start = ((f32[2,32,48,192]{3,2,1,0:T(8,128)}), f32[2,32,48,192]{3,2,1,0:T(8,128)}, u32[]{:S(2)}, u32[]{:S(2)}) async-start(f32[2,32,48,192]{3,2,1,0:T(8,128)} %copy.61), calls=%async_computation | async-start | bytes 6291456 | tf_op jit(solution)/shard_map/all_to_all | solution.py:39
  216.7 22.4 %all-to-all-start.5 = ((f32[32,48,128]{2,1,0:T(8,128)}), f32[32,48,128]{2,1,0:T(8,128)S(1)}, u32[]{:S(2)}, u32[]{:S(2)}) async-start(f32[32,48,128]{2,1,0:T(8,128)} %reduce_sum.38), calls=%async_computation.5 | async-start | bytes 1572864 | tf_op jit(solution)/shard_map/all_to_all | solution.py:47
  239.1 26.9 %all-to-all-start.1 = ((f32[32,48,192]{2,1,0:T(8,128)}), f32[32,48,192]{2,1,0:T(8,128)}, u32[]{:S(2)}, u32[]{:S(2)}) async-start(f32[32,48,192]{2,1,0:T(8,128)} %reduce_sum.36), calls=%async_computation.1 | async-start | bytes 3145728 | tf_op jit(solution)/shard_map/all_to_all | solution.py:47
  267.0 18.8 %all-to-all-start.6 = ((f32[32,48,128]{2,1,0:T(8,128)}), f32[32,48,128]{2,1,0:T(8,128)S(1)}, u32[]{:S(2)}, u32[]{:S(2)}) async-start(f32[32,48,128]{2,1,0:T(8,128)} %broadcast_in_dim.28), calls=%async_computation.6 | async-start | bytes 1572864 | tf_op jit(solution)/shard_map/all_to_all | solution.py:60
  336.6 39.8 %all-to-all-start.3 = ((f32[2,32,48,192]{3,2,1,0:T(8,128)}), f32[2,32,48,192]{3,2,1,0:T(8,128)}, u32[]{:S(2)}, u32[]{:S(2)}) async-start(f32[2,32,48,192]{3,2,1,0:T(8,128)} %broadcast_in_dim.27), calls=%async_computation.3 | async-start | bytes 6291456 | tf_op jit(solution)/shard_map/all_to_all | solution.py:60
  437.2 14.2 %copy-start.5 = (f32[6,256,256]{2,1,0:T(8,128)S(1)}, f32[6,256,256]{2,1,0:T(8,128)}, u32[]{:S(2)}) copy-start(f32[6,256,256]{2,1,0:T(8,128)} %copy-done.3) | copy-start | bytes 4718596
  437.3 8.0 %collective-permute-start.6 = (f32[1,256,128]{2,1,0:T(8,128)S(1)}, f32[1,256,128]{2,1,0:T(8,128)S(1)}, u32[]{:S(2)}, u32[]{:S(2)}) collective-permute-start(f32[1,256,128]{2,1,0:T(8,128)S(1)} %get-tuple-element.38), channel_id=1, source_target_pairs={{0,64},{64,128},{128,192},{192,0},{1,65},{65,129},{129,193},{193,1... | collective-permute-start | bytes 393224 | tf_op jit(solution)/shard_map/ppermute | solution.py:23
  438.5 10.3 %collective-permute-start.7 = (f32[1,256,128]{2,1,0:T(8,128)S(1)}, f32[1,256,128]{2,1,0:T(8,128)S(1)}, u32[]{:S(2)}, u32[]{:S(2)}) collective-permute-start(f32[1,256,128]{2,1,0:T(8,128)S(1)} %get-tuple-element.37), channel_id=1, source_target_pairs={{64,0},{128,64},{192,128},{0,192},{65,1},{129,65},{193,129},{1,193... | collective-permute-start | bytes 393224 | tf_op jit(solution)/shard_map/ppermute | solution.py:26
  440.9 7.9 %collective-permute-start.8 = (f32[1,256,128]{2,1,0:T(8,128)S(1)}, f32[1,256,128]{2,1,0:T(8,128)S(1)}, u32[]{:S(2)}, u32[]{:S(2)}) collective-permute-start(f32[1,256,128]{2,1,0:T(8,128)S(1)} %get-tuple-element.36), channel_id=1, source_target_pairs={{0,8},{8,16},{16,24},{24,32},{32,40},{40,48},{48,56},{56,0},{1,9},... | collective-permute-start | bytes 393224 | tf_op jit(solution)/shard_map/ppermute | solution.py:23
  445.2 4.4 collective-permute-start.9
  445.2 6.2 %collective-permute-start.10 = (f32[1,256,128]{2,1,0:T(8,128)S(1)}, f32[1,256,128]{2,1,0:T(8,128)S(1)}, u32[]{:S(2)}, u32[]{:S(2)}) collective-permute-start(f32[1,256,128]{2,1,0:T(8,128)S(1)} %get-tuple-element.34), channel_id=1, source_target_pairs={{0,1},{1,2},{2,3},{3,4},{4,5},{5,6},{6,7},{7,0},{8,9},{9,10},{10,1... | collective-permute-start | bytes 393224 | tf_op jit(solution)/shard_map/ppermute | solution.py:23
  445.2 6.1 %collective-permute-start.11 = (f32[1,256,128]{2,1,0:T(8,128)S(1)}, f32[1,256,128]{2,1,0:T(8,128)S(1)}, u32[]{:S(2)}, u32[]{:S(2)}) collective-permute-start(f32[1,256,128]{2,1,0:T(8,128)S(1)} %get-tuple-element.33), channel_id=1, source_target_pairs={{1,0},{2,1},{3,2},{4,3},{5,4},{6,5},{7,6},{0,7},{9,8},{10,9},{11,1... | collective-permute-start | bytes 393224 | tf_op jit(solution)/shard_map/ppermute | solution.py:26
  451.4 2.5 copy-start.1
where the time goes:
time: 463 us; the launch traced here: 454 us
  other arithmetic  125 us (27%)
  waiting for transfers between devices  113 us (24%)
  starting transfers between devices  60.4 us (13%)
  local copies, waits for them, and re-layouts  56.6 us (12%)
  blocking collectives  48.5 us (10%)
  matrix products  48.3 us (10%)
    all_to_all x2, blocking collectives, copy_for_each(): return lax.all_to_all(copies, axis, split_axis=0, concat_axis=0, tiled=True)  48.5 us
    all_to_all x2, waiting for transfers between devices, copy_for_each(): return lax.all_to_all(copies, axis, split_axis=0, concat_axis=0, tiled=True)  42.6 us
    another operation x7, other arithmetic, subspace(): factor = jnp.linalg.cholesky(gram)  35.5 us
    all_to_all x2, waiting for transfers between devices, sum_at_owner(): lax.all_to_all(in_blocks(shard, dim, devices), axis, 0, 0, tiled=True)  32.8 us
    all_to_all x2, waiting for transfers between devices, summed_rows(): lax.all_to_all(nearer, far, split_axis=0, concat_axis=0, tiled=True)  31.4 us
    another operation x5, other arithmetic, right_factor(): return jax.scipy.linalg.solve_triangular(factor, image.T, lower=True).T  29.7 us
    another operation x7, other arithmetic, solve_one(): factor = jnp.linalg.cholesky(matrix)  28.9 us
    unnamed x38, local copies, waits for them, and re-layouts  21 us
  transfers between devices with their start and end apart: 18, of which 9 were waited for; matrix products, arithmetic and copies ran while one was open for 11% of the time, Pallas kernels for 0%

commit v1 on v0

v1 whole, which is shorter than its diff:
```python
import functools

import jax
import jax.numpy as jnp
from jax import lax
from jax.experimental import pallas as pl
from jax.experimental.pallas import tpu as pltpu
from jax.sharding import PartitionSpec as P

FACE = 256
NCON = 32
COLS = 128
FACES = 6
ORDER = FACE * FACES
COARSE = NCON * FACES
SUB_ITERS = 2
GX, GY, GZ = 4, 8, 8
MESH = pl.DeviceIdType.MESH
NN = (((1,), (0,)), ((), ()))
NT = (((1,), (1,)), ((), ()))
F32 = jnp.float32
BF16 = jnp.bfloat16
ANY = pl.BlockSpec(memory_space=pl.ANY)
VMEM = pl.BlockSpec(memory_space=pltpu.VMEM)
SMEM = pl.BlockSpec(memory_space=pltpu.SMEM)


def here():
    return lax.axis_index("gx"), lax.axis_index("gy"), lax.axis_index("gz")


def across(face):
    gx, gy, gz = here()
    step = 1 if face % 2 else -1
    if face < 2:
        return lax.rem(gx + step + GX, GX), gy, gz
    if face < 4:
        return gx, lax.rem(gy + step + GY, GY), gz
    return gx, gy, lax.rem(gz + step + GZ, GZ)


def greet(devices):
    barrier = pltpu.get_barrier_semaphore()
    for device in devices:
        pl.semaphore_signal(barrier, inc=1, device_id=device, device_id_type=MESH)
    pl.semaphore_wait(barrier, len(devices))


def send(src, dst, send_sem, recv_sem, device):
    return pltpu.make_async_remote_copy(
        src_ref=src,
        dst_ref=dst,
        send_sem=send_sem,
        recv_sem=recv_sem,
        device_id=device,
        device_id_type=MESH,
    )


def split(value):
    high = value.astype(BF16)
    return high, (value - high.astype(F32)).astype(BF16)


def product(left, right, dims=NN):
    (left_high, left_low), (right_high, right_low) = left, right
    rows = left_high.shape[0]
    both = lax.dot_general(
        jnp.concatenate([left_high, left_low], axis=0),
        right_high,
        dims,
        preferred_element_type=F32,
    )
    cross = lax.dot_general(left_high, right_low, dims, preferred_element_type=F32)
    return both[:rows] + (both[rows:] + cross)


def faces_kernel(schur, partner, send_sem, recv_sem):
    greet([across(f) for f in range(FACES)])
    copies = []
    for f in range(FACES):
        block = pl.ds(f * FACE, FACE)
        copy = send(
            schur.at[block, block],
            partner.at[f ^ 1],
            send_sem.at[f],
            recv_sem.at[f ^ 1],
            across(f),
        )
        copy.start()
        copies.append(copy)
    for copy in copies:
        copy.wait()


def lane(value, index):
    return jnp.broadcast_to(value[:, index : index + 1], value.shape)


def local_kernel(
    schur_hbm, partner, start, resid, item, basis_out, inverse_out, side_out,
    schur, own_high, own_low, part_high, part_low, x_high, x_low, rows, image, lower, wide,
    load_sem,
):
    loads = []
    for f in range(FACES):
        block = pl.ds(f * FACE, FACE)
        copy = pltpu.make_async_copy(schur_hbm.at[block, :], schur.at[block, :], load_sem.at[f])
        copy.start()
        loads.append(copy)
    for copy in loads:
        copy.wait()
    row_ids = lax.broadcasted_iota(jnp.int32, (FACE, FACE), 0)
    col_ids = lax.broadcasted_iota(jnp.int32, (FACE, FACE), 1)

    def invert(f):
        block = pl.ds(pl.multiple_of(f * FACE, FACE), FACE)
        own = schur[block, block]
        other = partner[f]
        own_high[f], own_low[f] = split(own)
        part_high[f], part_low[f] = split(other)
        total = own + other
        diagonal = jnp.where(row_ids == col_ids, total, 0.0)
        across_row = 1.0 / jnp.sum(diagonal, axis=0, keepdims=True)
        down_col = 1.0 / jnp.sum(diagonal, axis=1, keepdims=True)
        total_parts = split(total)
        x = jnp.where(row_ids == col_ids, 2.0 * across_row, 0.0) - total * across_row * down_col
        for _ in range(2):
            x_parts = split(x)
            x = 2.0 * x - product(x_parts, split(product(total_parts, x_parts)))
        inverse_out[f] = x
        x_high[f], x_low[f] = split(x)

    def invert_pair(axis, carry):
        invert(2 * axis)
        invert(2 * axis + 1)
        return carry

    lax.fori_loop(0, 3, invert_pair, 0)
    for f in range(FACES):
        basis_out[f] = start[f].T
    rows[...] = jnp.zeros_like(rows)
    small_row = lax.broadcasted_iota(jnp.int32, (NCON, 2 * NCON), 0)
    small_col = lax.broadcasted_iota(jnp.int32, (NCON, 2 * NCON), 1)
    identity = jnp.where(small_row == small_col, 1.0, 0.0)

    def iterate(_, carry):
        for f in range(FACES):
            value = product(split(basis_out[f]), (part_high[f], part_low[f]))
            value = product(split(value), (x_high[f], x_low[f]))
            value = product(split(value), (own_high[f], own_low[f]))
            image[f] = value
            high, low = split(value)
            blank = jnp.zeros_like(high)
            shifted = (
                jnp.concatenate([blank, high], axis=0),
                jnp.concatenate([blank, low], axis=0),
            )
            gram = product((high, low), shifted, NT) + identity
            rows[pl.ds(f, NCON, stride=8), 0 : 2 * NCON] = gram
        work = [rows[8 * i : 8 * i + 8, :] for i in range(NCON)]
        for j in range(NCON):
            pivot = lane(work[j], NCON + j)
            scaled = work[j] * (1.0 / pivot)
            for i in range(j + 1, NCON):
                work[i] = work[i] - lane(work[j], NCON + i) * scaled
            rows[8 * j : 8 * j + 8, :] = work[j] * lax.rsqrt(pivot)
        for f in range(FACES):
            factor = rows[pl.ds(f, NCON, stride=8), 0:NCON]
            basis_out[f] = product(split(factor), split(image[f]))
        return carry

    lax.fori_loop(0, SUB_ITERS, iterate, 0)

    wide[...] = jnp.zeros_like(wide)
    for f in range(FACES):
        wide[f * NCON : (f + 1) * NCON, f * FACE : (f + 1) * FACE] = basis_out[f]

    def coarse_rows(f, carry):
        parts = split(basis_out[f])
        block = pl.ds(pl.multiple_of(f * FACE, FACE), FACE)
        out = pl.ds(pl.multiple_of(f * NCON, NCON), NCON)
        for g in range(FACES):
            lower[out, g * FACE : (g + 1) * FACE] = product(
                parts, split(schur[block, g * FACE : (g + 1) * FACE])
            )
        item[1, out, :] = product(parts, split(resid[block, :]))
        side = product(parts, (own_high[f], own_low[f]))
        side_out[f] = product(split(side), (x_high[f], x_low[f]))
        return carry

    lax.fori_loop(0, FACES, coarse_rows, 0)
    coarse = product(split(lower[...]), split(wide[...]), NT)
    item[0, 0:64, 0:64] = coarse[0:64, 0:64]
    item[0, 0:64, 64:128] = coarse[128:192, 128:192]
    item[0, 64:192, :] = coarse[64:192, 0:128]


def gather_kernel(
    group_of, item, basis, total, partner_basis,
    held, partial, arrived, passed, send_sem, recv_sem, basis_send, basis_recv,
):
    gx, gy, gz = here()
    x, core = gy // 2, lax.rem(gy, 2)
    y, z = gz // 2, lax.rem(gz, 2)
    kind = core

    def ring(step):
        nx = lax.rem(x + (1 - core) * step, 4)
        ny = lax.rem(y + core * step, 4)
        return gx, 2 * nx + core, 2 * ny + z

    def other_ring(step):
        nx = lax.rem(x + core * step, 4)
        ny = lax.rem(y + (1 - core) * step, 4)
        return gx, 2 * nx + core, 2 * ny + z

    mate = (gx, 2 * x + (1 - core), gz)
    over = (gx, gy, 2 * y + (1 - z))
    targets = [mate, over] + [ring(s) for s in (1, 3)] + [other_ring(s) for s in (1, 2, 3)]
    greet(targets + [across(f) for f in range(FACES)])

    half = COARSE // 2
    counter = [0]

    def copy(src, dst, device):
        n = counter[0]
        counter[0] += 1
        return send(src, dst, send_sem.at[n], recv_sem.at[n], device)

    swap = copy(item.at[1 - kind], held.at[0, 0, 1], mate)
    swap.start()
    own_over = copy(item.at[kind], held.at[0, 1, 0], over)
    own_over.start()
    pending = [swap, own_over]
    first = {}

    def spread(src, zz, cc):
        up = copy(src, held.at[1, zz, cc], ring(1))
        up.start()
        down = copy(src, held.at[3, zz, cc], ring(3))
        down.start()
        first[zz, cc] = (up, down)

    def relay(zz, cc):
        up, down = first[zz, cc]
        up.wait_recv()
        low = copy(
            held.at[1, zz, cc, pl.ds(0, half), :], held.at[2, zz, cc, pl.ds(0, half), :], ring(1)
        )
        low.start()
        down.wait_recv()
        high = copy(
            held.at[3, zz, cc, pl.ds(half, half), :], held.at[2, zz, cc, pl.ds(half, half), :],
            ring(3),
        )
        high.start()
        pending.extend([low, high])

    spread(item.at[kind], 0, 0)
    swap.wait_recv()
    mate_over = copy(held.at[0, 0, 1], held.at[0, 1, 1], over)
    mate_over.start()
    pending.append(mate_over)
    spread(held.at[0, 0, 1], 0, 1)
    basis_copies = []
    for f in range(FACES):
        c = send(basis.at[f], partner_basis.at[f ^ 1], basis_send.at[f], basis_recv.at[f ^ 1], across(f))
        c.start()
        basis_copies.append(c)
    own_over.wait_recv()
    spread(held.at[0, 1, 0], 1, 0)
    mate_over.wait_recv()
    spread(held.at[0, 1, 1], 1, 1)
    relay(0, 0)
    relay(0, 1)
    relay(1, 0)
    relay(1, 1)
    for c in pending[3:]:
        c.wait_recv()
    for c in pending:
        c.wait_send()
    for up, down in first.values():
        up.wait_send()
        down.wait_send()

    def group_at(place, cc, flip=0):
        _, gy_at, gz_at = place
        gy_at = gy_at + cc * (1 - 2 * core)
        gz_at = gz_at + flip * (1 - 2 * z)
        return group_of[gy_at * GZ + gz_at]

    sources = [
        (ring((4 - s // 4) % 4), s % 2, (s // 2) % 2) for s in range(16)
    ]
    out_copies = []
    for step in (1, 2, 3, 0):
        for cc in (0, 1):
            goal = group_at(other_ring(step), cc)
            coefs = [jnp.where(group_at(*s) == goal, 1.0, 0.0) for s in sources]

            def add_rows(r, carry):
                block = pl.ds(pl.multiple_of(r * 16, 16), 16)
                acc = None
                for s in range(16):
                    if s == 0:
                        piece = item[kind, block, :]
                    else:
                        piece = held[s // 4, (s // 2) % 2, s % 2, block, :]
                    term = coefs[s] * piece
                    acc = term if acc is None else acc + term
                partial[step, cc, block, :] = acc
                return carry

            lax.fori_loop(0, COARSE // 16, add_rows, 0)
        if step:
            c = copy(partial.at[step], arrived.at[step - 1], other_ring(step))
            c.start()
            out_copies.append(c)
    for c in out_copies:
        c.wait_recv()
    passed[...] = partial[0, 1] + arrived[0, 1] + arrived[1, 1] + arrived[2, 1]
    last = copy(passed, total.at[kind], mate)
    last.start()
    mine = partial[0, 0] + arrived[0, 0] + arrived[1, 0] + arrived[2, 0]
    total[kind] = mine
    for c in out_copies:
        c.wait_send()
    last.wait()
    for c in basis_copies:
        c.wait()


def exact(left, right):
    return lax.dot_general(
        left, right, NN, precision=lax.Precision.HIGHEST, preferred_element_type=F32
    )


def solve_kernel(total, partner_basis, partner, inverse, side, answer, mixed, system, rows):
    def mix(f, carry):
        value = product(split(partner_basis[f]), split(partner[f]))
        value = product(split(value), split(inverse[f]))
        mixed[f] = jnp.concatenate([side[f], value], axis=0).T
        return carry

    lax.fori_loop(0, FACES, mix, 0)
    system[:, 0:COLS] = total[1]
    packed = total[0]
    corner = packed[0:64, 64:128]
    first = packed[0:64, 0:64]
    below = packed[64:192, 0:64]
    middle = packed[64:128, 64:128]
    last = packed[128:192, 64:128]
    system[0:64, COLS : COLS + 192] = jnp.concatenate([first, below.T], axis=1)
    system[64:192, COLS : COLS + 192] = jnp.concatenate(
        [
            below,
            jnp.concatenate([middle, last], axis=0),
            jnp.concatenate([last.T, corner], axis=0),
        ],
        axis=1,
    )
    rows[...] = jnp.zeros_like(rows)
    small_row = lax.broadcasted_iota(jnp.int32, (NCON, NCON), 0)
    small_col = lax.broadcasted_iota(jnp.int32, (NCON, NCON), 1)
    identity = jnp.where(small_row == small_col, 1.0, 0.0)
    tall = lax.broadcasted_iota(jnp.int32, (COARSE, NCON), 0)
    for k in range(FACES):
        r0 = k * NCON
        block = system[r0 : r0 + NCON, COLS + r0 : COLS + r0 + NCON]
        rows[pl.ds(0, NCON, stride=8), 0 : 2 * NCON] = jnp.concatenate([identity, block], axis=1)
        work = [rows[8 * i : 8 * i + 8, :] for i in range(NCON)]
        for j in range(NCON):
            scaled = work[j] * (1.0 / lane(work[j], NCON + j))
            for i in range(NCON):
                if i > j:
                    work[i] = work[i] - lane(work[j], NCON + i) * scaled
                elif i < j:
                    work[i] = work[i] + lane(work[j], i) * scaled
            work[j] = scaled
        for i in range(NCON):
            rows[8 * i : 8 * i + 8, :] = work[i]
        pivot_inverse = rows[pl.ds(0, NCON, stride=8), 0:NCON]
        column = system[:, COLS + r0 : COLS + r0 + NCON]
        column = jnp.where((tall >= r0) & (tall < r0 + NCON), 0.0, column)
        scaled_rows = exact(pivot_inverse, system[r0 : r0 + NCON, :])
        system[...] = system[...] - exact(column, scaled_rows)
        system[r0 : r0 + NCON, :] = scaled_rows
    answer[...] = system[:, 0:COLS].reshape(FACES, NCON, COLS)


def answers_kernel(answer, partner_answer, send_sem, recv_sem):
    greet([across(f) for f in range(FACES)])
    copies = []
    for f in range(FACES):
        copy = send(
            answer.at[f], partner_answer.at[f ^ 1], send_sem.at[f], recv_sem.at[f ^ 1], across(f)
        )
        copy.start()
        copies.append(copy)
    for copy in copies:
        copy.wait()


def final_kernel(mixed, answer, partner_answer, correction):
    for f in range(FACES):
        both = jnp.concatenate([answer[f], partner_answer[f]], axis=0)
        correction[f * FACE : (f + 1) * FACE, :] = product(split(mixed[f]), split(both))


def array(*shape):
    return jax.ShapeDtypeStruct(shape, F32)


def remote(collective_id):
    return pltpu.CompilerParams(collective_id=collective_id, has_side_effects=True)


DMA = pltpu.SemaphoreType.DMA


def per_device(schur, start_block, resid, group_of):
    matrix = schur[0, 0, 0]
    partner = pl.pallas_call(
        faces_kernel,
        out_shape=array(FACES, FACE, FACE),
        in_specs=[ANY],
        out_specs=ANY,
        scratch_shapes=[DMA((FACES,)), DMA((FACES,))],
        compiler_params=remote(0),
        name="faces",
    )(matrix)
    blocks = (FACES, FACE, FACE)
    item, basis, inverse, side = pl.pallas_call(
        local_kernel,
        out_shape=(
            array(2, COARSE, COLS),
            array(FACES, NCON, FACE),
            array(*blocks),
            array(FACES, NCON, FACE),
        ),
        in_specs=[ANY, VMEM, VMEM, VMEM],
        out_specs=(VMEM,) * 4,
        scratch_shapes=[pltpu.VMEM((ORDER, ORDER), F32)]
        + [pltpu.VMEM(blocks, BF16)] * 6
        + [
            pltpu.VMEM((8 * NCON, 128), F32),
            pltpu.VMEM((FACES, NCON, FACE), F32),
            pltpu.VMEM((COARSE, ORDER), F32),
            pltpu.VMEM((COARSE, ORDER), F32),
            DMA((FACES,)),
        ],
        name="local",
    )(matrix, partner, start_block[0, 0, 0], resid[0, 0, 0])
    total, partner_basis = pl.pallas_call(
        gather_kernel,
        out_shape=(array(2, COARSE, COLS), array(FACES, NCON, FACE)),
        in_specs=[SMEM, VMEM, VMEM],
        out_specs=(VMEM, VMEM),
        scratch_shapes=[
            pltpu.VMEM((4, 2, 2, COARSE, COLS), F32),
            pltpu.VMEM((4, 2, COARSE, COLS), F32),
            pltpu.VMEM((3, 2, COARSE, COLS), F32),
            pltpu.VMEM((COARSE, COLS), F32),
            DMA((23,)),
            DMA((23,)),
            DMA((FACES,)),
            DMA((FACES,)),
        ],
        compiler_params=remote(1),
        name="gather",
    )(group_of, item, basis)
    answer, mixed = pl.pallas_call(
        solve_kernel,
        out_shape=(array(FACES, NCON, COLS), array(FACES, FACE, 2 * NCON)),
        in_specs=[VMEM] * 5,
        out_specs=(VMEM, VMEM),
        scratch_shapes=[
            pltpu.VMEM((COARSE, 384), F32),
            pltpu.VMEM((8 * NCON, 128), F32),
        ],
        name="solve",
    )(total, partner_basis, partner, inverse, side)
    partner_answer = pl.pallas_call(
        answers_kernel,
        out_shape=array(FACES, NCON, COLS),
        in_specs=[VMEM],
        out_specs=VMEM,
        scratch_shapes=[DMA((FACES,)), DMA((FACES,))],
        compiler_params=remote(2),
        name="answers",
    )(answer)
    correction = pl.pallas_call(
        final_kernel,
        out_shape=array(ORDER, COLS),
        in_specs=[VMEM] * 3,
        out_specs=VMEM,
        name="final",
    )(mixed, answer, partner_answer)
    return correction[None, None, None]


def solution(mesh):
    in_specs = (
        P("gx", "gy", "gz", None, None),
        P("gx", "gy", "gz", None, None, None),
        P("gx", "gy", "gz", None, None),
        P(),
    )
    out_specs = P("gx", "gy", "gz", None, None)
    return jax.shard_map(
        per_device, mesh=mesh, in_specs=in_specs, out_specs=out_specs, check_vma=False
    )
```

time: 463 us -> 132 us (0.29); the launches traced: 454 us -> 132 us
  Pallas kernels: 0 us -> 129 us
  other arithmetic: 125 us -> 0 us
  waiting for transfers between devices: 113 us -> 0 us
  starting transfers between devices: 60.4 us -> 0 us
  local copies, waits for them, and re-layouts: 56.6 us -> 2.08 us
  blocking collectives: 48.5 us -> 0 us
  matrix products: 48.3 us -> 0 us
    pallas_call x0 -> x6, Pallas kernels: none -> 129 us  [the longest x1 33.6 us: per_device(): pl.pallas_call(faces_kernel, out_shape=array(FACES, FACE, FACE), in_specs...]
    another operation x26 -> x0, other arithmetic: 114 us -> none  [the longest x7 35.5 us: subspace(): factor = jnp.linalg.cholesky(gram)]
    all_to_all x6 -> x0, waiting for transfers between devices: 107 us -> none  [the longest x2 42.6 us: copy_for_each(): return lax.all_to_all(copies, axis, split_axis=0, concat_axis=0, tiled=True)]
    all_to_all x2 -> x0, blocking collectives: 48.5 us -> none  [copy_for_each(): return lax.all_to_all(copies, axis, split_axis=0, concat_axis=0, tiled=True)]
    dot_general x22 -> x0, matrix products: 45.8 us -> none  [the longest x1 7.91 us: per_device(): jnp.einsum('igj,gjc->igc', rows_grouped, basis, precision=precise)]
    all_to_all x6 -> x0, starting transfers between devices: 34.8 us -> none  [the longest x2 14.4 us: summed_rows(): lax.all_to_all(nearer, far, split_axis=0, concat_axis=0, tiled=True)]
    ppermute x12 -> x0, starting transfers between devices: 25.6 us -> none  [the longest x6 13.5 us: extended(): lax.ppermute(lax.slice_in_dim(block, 0, width, axis=dim), axis, backward)]
    unnamed x38 -> x1, local copies, waits for them, and re-layouts: 21 us -> 2.08 us
  transfers between devices with their start and end apart: 18 -> 0, of which waited for: 9 -> 0; matrix products, arithmetic and copies ran while one was open for 11% -> 0% of each run, Pallas kernels for 0% -> 0%
where the time goes in v1:
time: 132 us
  Pallas kernels  129 us (98%)
  local copies, waits for them, and re-layouts  2.08 us (2%)
    pallas_call x1, Pallas kernels, per_device(): pl.pallas_call(faces_kernel, out_shape=array(FACES, FACE, FACE), in_specs...  33.6 us
    pallas_call x1, Pallas kernels, per_device(): pl.pallas_call(gather_kernel, out_shape=(array(2, COARSE, COLS), array(FA...  29.9 us
    pallas_call x1, Pallas kernels, per_device(): pl.pallas_call(local_kernel, out_shape=(array(2, COARSE, COLS), array(FAC...  29.7 us
    pallas_call x1, Pallas kernels, per_device(): pl.pallas_call(solve_kernel, out_shape=(array(FACES, NCON, COLS), array(F...  26.6 us
    pallas_call x1, Pallas kernels, per_device(): pl.pallas_call(answers_kernel, out_shape=array(FACES, NCON, COLS), in_spe...  7.15 us

profile of v1, /device:TPU:1, one launch (start us, length us, event | category | flops | bytes accessed | tf_op | source)
XLA Modules:
  0.0 131.6 jit_solution(3378750565021775811)
XLA Ops:
  0.0 2.1 %copy.5 = f32[1,1,1,6,256,32]{5,4,3,2,1,0:T(8,128)} copy(f32[1,1,1,6,256,32]{4,5,3,2,1,0:T(8,128)} %param.5) | data formatting | bytes 393216 | tf_op args[1]
  2.1 33.6 %faces.1.partner = f32[6,256,256]{2,1,0:T(8,128)} custom-call(f32[1536,1536]{1,0:T(8,128)} %bitcast.4), custom_call_target="tpu_custom_call" | custom-call | tf_op jit(solution)/shard_map/faces/pallas_call | solution.py:425
  35.7 29.7 %local.1 = (f32[2,192,128]{2,1,0:T(8,128)}, f32[6,32,256]{2,1,0:T(8,128)}, f32[6,256,256]{2,1,0:T(8,128)}, f32[6,32,256]{2,1,0:T(8,128)}) custom-call(f32[1536,1536]{1,0:T(8,128)} %bitcast.5, f32[6,256,256]{2,1,0:T(8,128)} %faces.1.partner, f32[6,256,32]{2,1,0:T(8,128)} %bitcast.6, f32[1536,128]{1,0:T(8,128)} %bitcast.7), custom_call_target="tpu_custom_call" | custom-call | tf_op jit(solution)/shard_map/local/pallas_call | solution.py:435
  65.4 29.9 %gather.1 = (f32[2,192,128]{2,1,0:T(8,128)}, f32[6,32,256]{2,1,0:T(8,128)}) custom-call(s32[64]{0:T(128)} %group_of.1, f32[2,192,128]{2,1,0:T(8,128)} %get-tuple-element.13.item, f32[6,32,256]{2,1,0:T(8,128)} %get-tuple-element.14.basis), custom_call_target="tpu_custom_call" | custom-call | tf_op jit(solution)/shard_map/gather/pallas_call | solution.py:456
  95.3 26.6 %solve.1 = (f32[6,32,128]{2,1,0:T(8,128)}, f32[6,256,64]{2,1,0:T(8,128)}) custom-call(f32[2,192,128]{2,1,0:T(8,128)} %get-tuple-element.15.total, f32[6,32,256]{2,1,0:T(8,128)} %get-tuple-element.16.partner_basis, f32[6,256,256]{2,1,0:T(8,128)} %faces.1.partner, f32[6,256,256]{2,1,0:T(8,128)} %get-tuple-element.17.inverse, f32[6,32,256]{2,1,0:T(8,128)} %get-tuple-element.18.side), custom_call_target="tpu_custom_call" | custom-call | tf_op jit(solution)/shard_map/solve/pallas_call | solution.py:474
  121.9 7.2 %answers.1.partner_answer = f32[6,32,128]{2,1,0:T(8,128)} custom-call(f32[6,32,128]{2,1,0:T(8,128)} %get-tuple-element.20.answer), custom_call_target="tpu_custom_call" | custom-call | tf_op jit(solution)/shard_map/answers/pallas_call | solution.py:485
  129.1 2.5 %final.1 = f32[1536,128]{1,0:T(8,128)} custom-call(f32[6,256,64]{2,1,0:T(8,128)} %get-tuple-element.19.mixed, f32[6,32,128]{2,1,0:T(8,128)} %get-tuple-element.20.answer, f32[6,32,128]{2,1,0:T(8,128)} %answers.1.partner_answer), custom_call_target="tpu_custom_call" | custom-call | tf_op jit(solution)/shard_map/final/pallas_call | solution.py:494

commit v2 on v1

v2 whole, which is shorter than its diff:
```python
import functools

import jax
import jax.numpy as jnp
from jax import lax
from jax.experimental import pallas as pl
from jax.experimental.pallas import tpu as pltpu
from jax.sharding import PartitionSpec as P

FACE = 256
NCON = 32
COLS = 128
FACES = 6
ORDER = FACE * FACES
COARSE = NCON * FACES
SUB_ITERS = 2
GX, GY, GZ = 4, 8, 8
MESH = pl.DeviceIdType.MESH
NN = (((1,), (0,)), ((), ()))
NT = (((1,), (1,)), ((), ()))
F32 = jnp.float32
BF16 = jnp.bfloat16
ANY = pl.BlockSpec(memory_space=pl.ANY)
VMEM = pl.BlockSpec(memory_space=pltpu.VMEM)
SMEM = pl.BlockSpec(memory_space=pltpu.SMEM)


def here():
    return lax.axis_index("gx"), lax.axis_index("gy"), lax.axis_index("gz")


def across(face):
    gx, gy, gz = here()
    step = 1 if face % 2 else -1
    if face < 2:
        return lax.rem(gx + step + GX, GX), gy, gz
    if face < 4:
        return gx, lax.rem(gy + step + GY, GY), gz
    return gx, gy, lax.rem(gz + step + GZ, GZ)


def greet(devices):
    barrier = pltpu.get_barrier_semaphore()
    for device in devices:
        pl.semaphore_signal(barrier, inc=1, device_id=device, device_id_type=MESH)
    pl.semaphore_wait(barrier, len(devices))


def send(src, dst, send_sem, recv_sem, device):
    return pltpu.make_async_remote_copy(
        src_ref=src,
        dst_ref=dst,
        send_sem=send_sem,
        recv_sem=recv_sem,
        device_id=device,
        device_id_type=MESH,
    )


def split(value):
    high = value.astype(BF16)
    return high, (value - high.astype(F32)).astype(BF16)


def product(left, right, dims=NN):
    (left_high, left_low), (right_high, right_low) = left, right
    rows = left_high.shape[0]
    both = lax.dot_general(
        jnp.concatenate([left_high, left_low], axis=0),
        right_high,
        dims,
        preferred_element_type=F32,
    )
    cross = lax.dot_general(left_high, right_low, dims, preferred_element_type=F32)
    return both[:rows] + (both[rows:] + cross)


def faces_kernel(schur, partner, send_sem, recv_sem):
    greet([across(f) for f in range(FACES)])
    copies = []
    for f in range(FACES):
        block = pl.ds(f * FACE, FACE)
        copy = send(
            schur.at[block, block],
            partner.at[f ^ 1],
            send_sem.at[f],
            recv_sem.at[f ^ 1],
            across(f),
        )
        copy.start()
        copies.append(copy)
    for copy in copies:
        copy.wait()


def row_of(value, index):
    return jnp.broadcast_to(value[index : index + 1, :], value.shape)


def eliminate(systems, column_of, panel, inverse):
    sub = lax.broadcasted_iota(jnp.int32, (8, 128), 0)
    for first in range(0, NCON, panel):
        stop = first + panel
        low = 0 if inverse else first // 8
        spread = [
            {c: {v: column_of(slabs[v], c) for v in range(low, 4)} for c in range(first, stop)}
            for slabs in systems
        ]
        for j in range(first, stop):
            vj, sj = divmod(j, 8)
            for slabs, columns in zip(systems, spread):
                pivot = row_of(columns[j][vj], sj)
                invert = 1.0 / pivot
                row = row_of(slabs[vj], sj)
                scaled = row * invert
                rest = {c: row_of(columns[c][vj], sj) * invert for c in range(j + 1, stop)}
                done = scaled if inverse else row * lax.rsqrt(pivot)
                for v in range(0 if inverse else vj, 4):
                    factor = columns[j][v]
                    new = slabs[v] - factor * scaled
                    if v == vj:
                        new = jnp.where(sub == sj, done, new)
                        if not inverse and sj:
                            new = jnp.where(sub < sj, slabs[v], new)
                    slabs[v] = new
                    for c in range(j + 1, stop):
                        updated = columns[c][v] - factor * rest[c]
                        if inverse and v == vj:
                            updated = jnp.where(sub == sj, rest[c], updated)
                        columns[c][v] = updated


def local_kernel(
    schur_hbm, partner, start, resid, item, basis_out, inverse_out, side_out,
    schur, own_high, own_low, part_high, part_low, x_high, x_low, image, lower, wide,
    load_sem,
):
    loads = []
    for f in range(FACES):
        block = pl.ds(f * FACE, FACE)
        copy = pltpu.make_async_copy(schur_hbm.at[block, :], schur.at[block, :], load_sem.at[f])
        copy.start()
        loads.append(copy)
    for copy in loads:
        copy.wait()
    row_ids = lax.broadcasted_iota(jnp.int32, (FACE, FACE), 0)
    col_ids = lax.broadcasted_iota(jnp.int32, (FACE, FACE), 1)

    def invert(f):
        block = pl.ds(pl.multiple_of(f * FACE, FACE), FACE)
        own = schur[block, block]
        other = partner[f]
        own_high[f], own_low[f] = split(own)
        part_high[f], part_low[f] = split(other)
        total = own + other
        diagonal = jnp.where(row_ids == col_ids, total, 0.0)
        across_row = 1.0 / jnp.sum(diagonal, axis=0, keepdims=True)
        down_col = 1.0 / jnp.sum(diagonal, axis=1, keepdims=True)
        total_parts = split(total)
        x = jnp.where(row_ids == col_ids, 2.0 * across_row, 0.0) - total * across_row * down_col
        for _ in range(2):
            x_parts = split(x)
            x = 2.0 * x - product(x_parts, split(product(total_parts, x_parts)))
        inverse_out[f] = x
        x_high[f], x_low[f] = split(x)

    def invert_pair(axis, carry):
        invert(2 * axis)
        invert(2 * axis + 1)
        return carry

    lax.fori_loop(0, 3, invert_pair, 0)
    for f in range(FACES):
        basis_out[f] = start[f]
    lanes = lax.broadcasted_iota(jnp.int32, (NCON, 128), 1)
    down = lax.broadcasted_iota(jnp.int32, (NCON, 128), 0)
    identity = jnp.where(lax.rem(lanes, 64) == down, 1.0, 0.0)
    left_lanes = jnp.where(lanes < NCON, 1.0, 0.0)
    right_lanes = jnp.where((lanes >= 64) & (lanes < 64 + NCON), 1.0, 0.0)
    half_base = 64 * (lax.broadcasted_iota(jnp.int32, (8, 128), 1) // 64)
    blank = jnp.zeros((NCON, FACE), BF16)

    def column_of(slab, c):
        return jnp.take_along_axis(slab, half_base + (NCON + c), axis=1)

    def iterate(_, carry):
        systems = []
        for f in range(FACES):
            value = product(split(basis_out[f]), (part_high[f], part_low[f]))
            value = product(split(value), (x_high[f], x_low[f]))
            value = product(split(value), (own_high[f], own_low[f]))
            image[f] = value
        for f in range(0, FACES, 2):
            one, two = split(image[f]), split(image[f + 1])
            gram = product(
                one, [jnp.concatenate([blank, part, blank, blank], axis=0) for part in one], NT
            )
            gram = gram + product(
                two, [jnp.concatenate([blank, blank, blank, part], axis=0) for part in two], NT
            )
            gram = gram + identity
            systems.append([gram[8 * v : 8 * v + 8] for v in range(4)])
        eliminate(systems, column_of, 4, False)
        for f in range(0, FACES, 2):
            factor = jnp.concatenate(systems[f // 2], axis=0)
            factor = jnp.concatenate([factor * left_lanes, factor * right_lanes], axis=0)
            one, two = split(image[f]), split(image[f + 1])
            both = product(
                split(factor),
                [jnp.concatenate([p, blank, q, blank], axis=0) for p, q in zip(one, two)],
            )
            basis_out[f] = both[:NCON]
            basis_out[f + 1] = both[NCON:]
        return carry

    lax.fori_loop(0, SUB_ITERS, iterate, 0)

    wide[...] = jnp.zeros_like(wide)
    for f in range(FACES):
        wide[f * NCON : (f + 1) * NCON, f * FACE : (f + 1) * FACE] = basis_out[f]

    lower[...] = jnp.zeros_like(lower)
    for f in range(FACES):
        parts = split(basis_out[f])
        block = slice(f * FACE, (f + 1) * FACE)
        out = slice(f * NCON, (f + 1) * NCON)
        for g in range(f):
            lower[out, g * FACE : (g + 1) * FACE] = product(
                parts, split(schur[block, g * FACE : (g + 1) * FACE])
            )
        side = product(parts, (own_high[f], own_low[f]))
        lower[out, block] = side
        item[1, out, :] = product(parts, split(resid[block, :]))
        side_out[f] = product(split(side), (x_high[f], x_low[f]))
    coarse = product(split(lower[...]), split(wide[...]), NT)
    item[0, 0:64, 0:64] = coarse[0:64, 0:64]
    item[0, 0:64, 64:128] = coarse[128:192, 128:192]
    item[0, 64:192, :] = coarse[64:192, 0:128]


def back_kernel(
    group_of, item, basis, partner, inverse, side, answer, mixed, partner_answer,
    held, partial, relayed, arrived, passed, total, partner_basis, system,
    send_sem, recv_sem, basis_send, basis_recv, answer_send, answer_recv,
):
    gx, gy, gz = here()
    x, core = gy // 2, lax.rem(gy, 2)
    y, z = gz // 2, lax.rem(gz, 2)
    kind = core

    def ring(step):
        nx = lax.rem(x + (1 - core) * step, 4)
        ny = lax.rem(y + core * step, 4)
        return gx, 2 * nx + core, 2 * ny + z

    def other_ring(step):
        nx = lax.rem(x + core * step, 4)
        ny = lax.rem(y + (1 - core) * step, 4)
        return gx, 2 * nx + core, 2 * ny + z

    mate = (gx, 2 * x + (1 - core), gz)
    over = (gx, gy, 2 * y + (1 - z))
    targets = [mate, over] + [ring(s) for s in (1, 3)] + [other_ring(s) for s in (1, 3)]
    greet(targets + [across(f) for f in range(FACES)])

    half = COARSE // 2
    counter = [0]

    def copy(src, dst, device):
        n = counter[0]
        counter[0] += 1
        started = send(src, dst, send_sem.at[n], recv_sem.at[n], device)
        started.start()
        return started

    def slot(step, zz, cc):
        return held.at[4 * step + 2 * zz + cc]

    swap = copy(item.at[1 - kind], slot(0, 0, 1), mate)
    own_over = copy(item.at[kind], slot(0, 1, 0), over)
    pending = [swap, own_over]
    first = {}

    def spread(src, zz, cc):
        first[zz, cc] = (
            copy(src, slot(1, zz, cc), ring(1)),
            copy(src, slot(3, zz, cc), ring(3)),
        )

    def relay(zz, cc):
        up, down = first[zz, cc]
        top, bottom = pl.ds(0, half), pl.ds(half, half)
        up.wait_recv()
        pending.append(
            copy(slot(1, zz, cc).at[top, :], slot(2, zz, cc).at[top, :], ring(1))
        )
        down.wait_recv()
        pending.append(
            copy(slot(3, zz, cc).at[bottom, :], slot(2, zz, cc).at[bottom, :], ring(3))
        )

    spread(item.at[kind], 0, 0)
    swap.wait_recv()
    mate_over = copy(slot(0, 0, 1), slot(0, 1, 1), over)
    pending.append(mate_over)
    spread(slot(0, 0, 1), 0, 1)
    basis_copies = []
    for f in range(FACES):
        c = send(
            basis.at[f], partner_basis.at[f ^ 1], basis_send.at[f], basis_recv.at[f ^ 1], across(f)
        )
        c.start()
        basis_copies.append(c)

    held[0] = item[kind]
    held[16] = jnp.zeros((COARSE, COLS), F32)

    def group_at(place, cc, flip=0):
        _, gy_at, gz_at = place
        gy_at = gy_at + cc * (1 - 2 * core)
        gz_at = gz_at + flip * (1 - 2 * z)
        return group_of[gy_at * GZ + gz_at]

    source_groups = [
        group_at(ring((4 - s // 4) % 4), s % 2, (s // 2) % 2) for s in range(16)
    ]
    members = {}
    for step in range(4):
        for cc in (0, 1):
            goal = group_at(other_ring(step), cc)
            slots = [jnp.int32(16)] * 4
            for s in range(16):
                hit = source_groups[s] == goal
                slots = [
                    jnp.where(hit, new, old)
                    for new, old in zip([jnp.int32(s)] + slots[:3], slots)
                ]
            members[step, cc] = slots

    own_over.wait_recv()
    spread(slot(0, 1, 0), 1, 0)
    mate_over.wait_recv()
    spread(slot(0, 1, 1), 1, 1)
    relay(0, 0)
    relay(0, 1)
    relay(1, 0)
    relay(1, 1)
    for c in pending[3:]:
        c.wait_recv()

    def gather_members(step):
        for cc in (0, 1):
            slots = members[step, cc]

            def add_rows(r, carry):
                block = pl.ds(pl.multiple_of(r * 32, 32), 32)
                low = held[slots[0], block, :] + held[slots[1], block, :]
                high = held[slots[2], block, :] + held[slots[3], block, :]
                partial[step, cc, block, :] = low + high
                return carry

            lax.fori_loop(0, COARSE // 32, add_rows, 0)

    top, bottom = pl.ds(0, half), pl.ds(half, half)
    gather_members(2)
    relay_up = copy(partial.at[2, :, top, :], relayed.at[0], other_ring(1))
    relay_down = copy(partial.at[2, :, bottom, :], relayed.at[1], other_ring(3))
    gather_members(1)
    up_two = copy(partial.at[1, :, bottom, :], arrived.at[0, :, bottom, :], other_ring(1))
    gather_members(3)
    down_two = copy(partial.at[3, :, top, :], arrived.at[1, :, top, :], other_ring(3))
    relay_up.wait_recv()
    partial[1, :, top, :] = partial[1, :, top, :] + relayed[0]
    up_one = copy(partial.at[1, :, top, :], arrived.at[0, :, top, :], other_ring(1))
    relay_down.wait_recv()
    partial[3, :, bottom, :] = partial[3, :, bottom, :] + relayed[1]
    down_one = copy(partial.at[3, :, bottom, :], arrived.at[1, :, bottom, :], other_ring(3))
    gather_members(0)
    sends = [relay_up, relay_down, up_two, down_two, up_one, down_one]
    for c in sends[2:]:
        c.wait_recv()
    passed[...] = partial[0, 1] + arrived[0, 1] + arrived[1, 1]
    last = copy(passed, total.at[kind], mate)
    total[kind] = partial[0, 0] + arrived[0, 0] + arrived[1, 0]
    for c in pending + sends:
        c.wait_send()
    for up, down in first.values():
        up.wait_send()
        down.wait_send()
    for c in basis_copies:
        c.wait()

    def mix(f, carry):
        value = product(split(partner_basis[f]), split(partner[f]))
        value = product(split(value), split(inverse[f]))
        mixed[f] = jnp.concatenate([side[f], value], axis=0).T
        return carry

    lax.fori_loop(0, FACES, mix, 0)
    last.wait()

    system[:, 0:COLS] = total[1]
    packed = total[0]
    row64 = lax.broadcasted_iota(jnp.int32, (64, 64), 0) // NCON
    col64 = lax.broadcasted_iota(jnp.int32, (64, 64), 1) // NCON

    def fill(block):
        return block + jnp.where(row64 > col64, block, 0.0).T

    one = packed[0:64, 0:64]
    below = packed[64:192, 0:64]
    middle = packed[64:128, 64:128]
    final = packed[128:192, 64:128]
    corner = packed[0:64, 64:128]
    blank = jnp.zeros((64, 64), F32)
    system[0:64, COLS : COLS + 256] = jnp.concatenate([fill(one), below.T, blank], axis=1)
    system[64:192, COLS : COLS + 256] = jnp.concatenate(
        [
            below,
            jnp.concatenate([fill(middle), final], axis=0),
            jnp.concatenate([final.T, fill(corner)], axis=0),
            jnp.zeros((128, 64), F32),
        ],
        axis=1,
    )
    lanes = lax.broadcasted_iota(jnp.int32, (NCON, 128), 1)
    down = lax.broadcasted_iota(jnp.int32, (NCON, 128), 0)
    tall_lane = lax.broadcasted_iota(jnp.int32, (COARSE, 128), 1)
    tall_row = lax.broadcasted_iota(jnp.int32, (COARSE, 128), 0)

    def placed(block, offset):
        parts = []
        if offset:
            parts.append(jnp.zeros((offset, block.shape[1]), block.dtype))
        parts.append(block)
        if offset + NCON < 128:
            parts.append(jnp.zeros((128 - NCON - offset, block.shape[1]), block.dtype))
        return jnp.concatenate(parts, axis=0)

    for k in range(FACES):
        rows = slice(k * NCON, (k + 1) * NCON)
        tile = slice(COLS + 128 * (k // 4), COLS + 128 * (k // 4) + 128)
        place = (k % 4) * NCON
        unit = (place + NCON) % 128
        in_unit = (lanes >= unit) & (lanes < unit + NCON)
        in_place = (lanes >= place) & (lanes < place + NCON)
        block = jnp.where(in_place, system[rows, tile], 0.0)
        block = jnp.where(lanes == down + unit, 1.0, block)
        slabs = [block[8 * v : 8 * v + 8] for v in range(4)]
        eliminate(
            [slabs],
            lambda slab, c, place=place: jnp.broadcast_to(
                slab[:, place + c : place + c + 1], slab.shape
            ),
            8,
            True,
        )
        pivot_inverse = jnp.where(in_unit, jnp.concatenate(slabs, axis=0), 0.0)
        scaled = product(
            split(pivot_inverse), [placed(part, unit) for part in split(system[rows, :])]
        )
        column = jnp.where(
            (tall_lane >= place)
            & (tall_lane < place + NCON)
            & ((tall_row < k * NCON) | (tall_row >= (k + 1) * NCON)),
            system[:, tile],
            0.0,
        )
        update = product(split(column), [placed(part, place) for part in split(scaled)])
        system[...] = system[...] - update
        system[rows, :] = scaled
    answer[...] = system[:, 0:COLS].reshape(FACES, NCON, COLS)
    copies = []
    for f in range(FACES):
        c = send(
            answer.at[f], partner_answer.at[f ^ 1], answer_send.at[f], answer_recv.at[f ^ 1],
            across(f),
        )
        c.start()
        copies.append(c)
    for c in copies:
        c.wait()


def final_kernel(mixed, answer, partner_answer, correction):
    for f in range(FACES):
        both = jnp.concatenate([answer[f], partner_answer[f]], axis=0)
        correction[f * FACE : (f + 1) * FACE, :] = product(split(mixed[f]), split(both))


def array(*shape):
    return jax.ShapeDtypeStruct(shape, F32)


def remote(collective_id):
    return pltpu.CompilerParams(collective_id=collective_id, has_side_effects=True)


DMA = pltpu.SemaphoreType.DMA


def per_device(schur, start_block, resid, group_of):
    matrix = schur[0, 0, 0]
    partner = pl.pallas_call(
        faces_kernel,
        out_shape=array(FACES, FACE, FACE),
        in_specs=[ANY],
        out_specs=ANY,
        scratch_shapes=[DMA((FACES,)), DMA((FACES,))],
        compiler_params=remote(0),
        name="faces",
    )(matrix)
    blocks = (FACES, FACE, FACE)
    item, basis, inverse, side = pl.pallas_call(
        local_kernel,
        out_shape=(
            array(2, COARSE, COLS),
            array(FACES, NCON, FACE),
            array(*blocks),
            array(FACES, NCON, FACE),
        ),
        in_specs=[ANY, VMEM, VMEM, VMEM],
        out_specs=(VMEM,) * 4,
        scratch_shapes=[pltpu.VMEM((ORDER, ORDER), F32)]
        + [pltpu.VMEM(blocks, BF16)] * 6
        + [
            pltpu.VMEM((FACES, NCON, FACE), F32),
            pltpu.VMEM((COARSE, ORDER), F32),
            pltpu.VMEM((COARSE, ORDER), F32),
            DMA((FACES,)),
        ],
        name="local",
    )(matrix, partner, jnp.swapaxes(start_block[0, 0, 0], 1, 2), resid[0, 0, 0])
    answer, mixed, partner_answer = pl.pallas_call(
        back_kernel,
        out_shape=(
            array(FACES, NCON, COLS),
            array(FACES, FACE, 2 * NCON),
            array(FACES, NCON, COLS),
        ),
        in_specs=[SMEM] + [VMEM] * 5,
        out_specs=(VMEM,) * 3,
        scratch_shapes=[
            pltpu.VMEM((17, COARSE, COLS), F32),
            pltpu.VMEM((4, 2, COARSE, COLS), F32),
            pltpu.VMEM((2, 2, COARSE // 2, COLS), F32),
            pltpu.VMEM((2, 2, COARSE, COLS), F32),
            pltpu.VMEM((COARSE, COLS), F32),
            pltpu.VMEM((2, COARSE, COLS), F32),
            pltpu.VMEM((FACES, NCON, FACE), F32),
            pltpu.VMEM((COARSE, 384), F32),
            DMA((26,)),
            DMA((26,)),
        ]
        + [DMA((FACES,))] * 4,
        compiler_params=remote(1),
        name="back",
    )(group_of, item, basis, partner, inverse, side)
    correction = pl.pallas_call(
        final_kernel,
        out_shape=array(ORDER, COLS),
        in_specs=[VMEM] * 3,
        out_specs=VMEM,
        name="final",
    )(mixed, answer, partner_answer)
    return correction[None, None, None]


def solution(mesh):
    in_specs = (
        P("gx", "gy", "gz", None, None),
        P("gx", "gy", "gz", None, None, None),
        P("gx", "gy", "gz", None, None),
        P(),
    )
    out_specs = P("gx", "gy", "gz", None, None)
    return jax.shard_map(
        per_device, mesh=mesh, in_specs=in_specs, out_specs=out_specs, check_vma=False
    )
```

time: 132 us -> 101 us (0.77)
  Pallas kernels: 129 us -> 99.9 us
  local copies, waits for them, and re-layouts: 2.08 us -> 0 us
    pallas_call x3 -> x1, Pallas kernels: 63.6 us -> 42.4 us  [per_device(): pl.pallas_call(back_kernel, out_shape=(array(FACES, NCON, COLS), array(FA...]
    pallas_call x1, Pallas kernels: 29.7 us -> 21.4 us  [per_device(): pl.pallas_call(local_kernel, out_shape=(array(2, COARSE, COLS), array(FAC...]
    unnamed x1 -> x0, local copies, waits for them, and re-layouts: 2.08 us -> none
where the time goes in v2:
time: 101 us; the launch traced here: 100 us
  Pallas kernels  99.9 us (99%)
    pallas_call x1, Pallas kernels, per_device(): pl.pallas_call(back_kernel, out_shape=(array(FACES, NCON, COLS), array(FA...  42.4 us
    pallas_call x1, Pallas kernels, per_device(): pl.pallas_call(faces_kernel, out_shape=array(FACES, FACE, FACE), in_specs...  33.6 us
    pallas_call x1, Pallas kernels, per_device(): pl.pallas_call(local_kernel, out_shape=(array(2, COARSE, COLS), array(FAC...  21.4 us
    pallas_call x1, Pallas kernels, per_device(): pl.pallas_call(final_kernel, out_shape=array(ORDER, COLS), in_specs=[VMEM...  2.53 us

profile of v2, /device:TPU:1, one launch (start us, length us, event | category | flops | bytes accessed | tf_op | source)
XLA Modules:
  0.0 100.0 jit_solution(17846359310285257029)
XLA Ops:
  0.0 33.6 %faces.1.partner = f32[6,256,256]{2,1,0:T(8,128)} custom-call(f32[1536,1536]{1,0:T(8,128)} %bitcast.6), custom_call_target="tpu_custom_call" | custom-call | tf_op jit(solution)/shard_map/faces/pallas_call | solution.py:504
  33.6 21.4 %local.1 = (f32[2,192,128]{2,1,0:T(8,128)}, f32[6,32,256]{2,1,0:T(8,128)}, f32[6,256,256]{2,1,0:T(8,128)}, f32[6,32,256]{2,1,0:T(8,128)}) custom-call(f32[1536,1536]{1,0:T(8,128)} %bitcast.7, f32[6,256,256]{2,1,0:T(8,128)} %faces.1.partner, f32[6,32,256]{2,1,0:T(8,128)} %bitcast.9, f32[1536,128]{1,0:T(8,128)} %bitcast.8), custom_call_target="tpu_custom_call" | custom-call | tf_op jit(solution)/shard_map/local/pallas_call | solution.py:514
  55.0 42.4 %back.1 = (f32[6,32,128]{2,1,0:T(8,128)}, f32[6,256,64]{2,1,0:T(8,128)}, f32[6,32,128]{2,1,0:T(8,128)}) custom-call(s32[64]{0:T(128)} %group_of.1, f32[2,192,128]{2,1,0:T(8,128)} %get-tuple-element.12.item, f32[6,32,256]{2,1,0:T(8,128)} %get-tuple-element.13.basis, f32[6,256,256]{2,1,0:T(8,128)} %faces.1.partner, f32[6,256,256]{2,1,0:T(8,128)} %get-tuple-element.14.inverse, ...), custom_call_target="tpu_custom_call" | custom-call | tf_op jit(solution)/shard_map/back/pallas_call | solution.py:534
  97.4 2.5 %final.1 = f32[1536,128]{1,0:T(8,128)} custom-call(f32[6,256,64]{2,1,0:T(8,128)} %get-tuple-element.16.mixed, f32[6,32,128]{2,1,0:T(8,128)} %get-tuple-element.17.answer, f32[6,32,128]{2,1,0:T(8,128)} %get-tuple-element.18.partner_answer), custom_call_target="tpu_custom_call" | custom-call | tf_op jit(solution)/shard_map/final/pallas_call | solution.py:559

commit v3 on v2

--- a/solution.py
+++ b/solution.py
@@ -73,24 +73,6 @@
     )
     cross = lax.dot_general(left_high, right_low, dims, preferred_element_type=F32)
     return both[:rows] + (both[rows:] + cross)
-
-
-def faces_kernel(schur, partner, send_sem, recv_sem):
-    greet([across(f) for f in range(FACES)])
-    copies = []
-    for f in range(FACES):
-        block = pl.ds(f * FACE, FACE)
-        copy = send(
-            schur.at[block, block],
-            partner.at[f ^ 1],
-            send_sem.at[f],
-            recv_sem.at[f ^ 1],
-            across(f),
-        )
-        copy.start()
-        copies.append(copy)
-    for copy in copies:
-        copy.wait()
 
 
 def row_of(value, index):
@@ -130,29 +112,91 @@
                         columns[c][v] = updated
 
 
-def local_kernel(
-    schur_hbm, partner, start, resid, item, basis_out, inverse_out, side_out,
-    schur, own_high, own_low, part_high, part_low, x_high, x_low, image, lower, wide,
-    load_sem,
+def front_kernel(
+    schur_hbm, start_hbm, resid_hbm, item, mixes,
+    schur, high, low, other, other_high, other_low, x_high, x_low, start, other_start, resid,
+    basis, lower, wide, send_sem, recv_sem, load_sem,
 ):
+    gx, gy, gz = here()
+    core = lax.rem(gy, 2)
+    turns = (core, 0, core)
+    mine = [2 * a + turns[a] for a in range(3)]
+    theirs = [2 * a + 1 - turns[a] for a in range(3)]
+
+    def along(a, step):
+        if a == 0:
+            return lax.rem(gx + step + GX, GX), gy, gz
+        if a == 1:
+            return gx, lax.rem(gy + step + GY, GY), gz
+        return gx, gy, lax.rem(gz + step + GZ, GZ)
+
+    ahead = [along(a, 1 - 2 * turns[a]) for a in range(3)]
+    behind = [along(a, 2 * turns[a] - 1) for a in range(3)]
+
+    def block(f, size=FACE):
+        return pl.ds(pl.multiple_of(f * size, size), size)
+
     loads = []
-    for f in range(FACES):
-        block = pl.ds(f * FACE, FACE)
-        copy = pltpu.make_async_copy(schur_hbm.at[block, :], schur.at[block, :], load_sem.at[f])
+
+    def load(src, dst):
+        copy = pltpu.make_async_copy(src, dst, load_sem.at[len(loads)])
         copy.start()
         loads.append(copy)
-    for copy in loads:
-        copy.wait()
+
+    for f in range(FACES):
+        rows = pl.ds(f * FACE, FACE)
+        load(schur_hbm.at[rows, :], schur.at[rows, :])
+    load(start_hbm, start)
+    load(resid_hbm, resid)
+    greet(ahead + behind)
+
+    def copy(n, src, dst, device):
+        started = send(src, dst, send_sem.at[n], recv_sem.at[n], device)
+        started.start()
+        return started
+
+    half = FACE // 2
+    faces = {}
+    for a in (0, 2, 1):
+        f = theirs[a]
+        corner = pl.ds(pl.multiple_of(f * FACE, FACE), half)
+        bottom = pl.ds(pl.multiple_of(f * FACE + half, half), half)
+        faces[a] = [
+            copy(
+                5 * a, schur_hbm.at[bottom, block(f)], other.at[a, pl.ds(half, half), :], ahead[a]
+            ),
+            copy(
+                5 * a + 1,
+                schur_hbm.at[corner, corner],
+                other.at[a, pl.ds(0, half), pl.ds(0, half)],
+                ahead[a],
+            ),
+            copy(5 * a + 2, start_hbm.at[f], other_start.at[a], ahead[a]),
+        ]
+
+    def divide(r, carry):
+        rows = pl.ds(pl.multiple_of(r * 64, 64), 64)
+        high[rows, :], low[rows, :] = split(schur[rows, :])
+        return carry
+
+    lower[...] = jnp.zeros_like(lower)
+    wide[...] = jnp.zeros_like(wide)
+    for f in range(FACES):
+        loads[f].wait()
+        lax.fori_loop(f * 4, f * 4 + 4, divide, 0)
+    loads[6].wait()
+    loads[7].wait()
+
     row_ids = lax.broadcasted_iota(jnp.int32, (FACE, FACE), 0)
     col_ids = lax.broadcasted_iota(jnp.int32, (FACE, FACE), 1)
 
-    def invert(f):
-        block = pl.ds(pl.multiple_of(f * FACE, FACE), FACE)
-        own = schur[block, block]
-        other = partner[f]
-        own_high[f], own_low[f] = split(own)
-        part_high[f], part_low[f] = split(other)
-        total = own + other
+    def invert(a):
+        for c in faces[a]:
+            c.wait_recv()
+        other[a, 0:half, half:FACE] = other[a, half:FACE, 0:half].T
+        theirs_block = other[a]
+        other_high[a], other_low[a] = split(theirs_block)
+        total = schur[block(mine[a]), block(mine[a])] + theirs_block
         diagonal = jnp.where(row_ids == col_ids, total, 0.0)
         across_row = 1.0 / jnp.sum(diagonal, axis=0, keepdims=True)
         down_col = 1.0 / jnp.sum(diagonal, axis=1, keepdims=True)
@@ -161,17 +205,12 @@
         for _ in range(2):
             x_parts = split(x)
             x = 2.0 * x - product(x_parts, split(product(total_parts, x_parts)))
-        inverse_out[f] = x
-        x_high[f], x_low[f] = split(x)
-
-    def invert_pair(axis, carry):
-        invert(2 * axis)
-        invert(2 * axis + 1)
-        return carry
-
-    lax.fori_loop(0, 3, invert_pair, 0)
-    for f in range(FACES):
-        basis_out[f] = start[f]
+        x_high[a], x_low[a] = split(x)
+
+    invert(1)
+    invert(2)
+    invert(0)
+
     lanes = lax.broadcasted_iota(jnp.int32, (NCON, 128), 1)
     down = lax.broadcasted_iota(jnp.int32, (NCON, 128), 0)
     identity = jnp.where(lax.rem(lanes, 64) == down, 1.0, 0.0)
@@ -183,15 +222,25 @@
     def column_of(slab, c):
         return jnp.take_along_axis(slab, half_base + (NCON + c), axis=1)
 
-    def iterate(_, carry):
-        systems = []
-        for f in range(FACES):
-            value = product(split(basis_out[f]), (part_high[f], part_low[f]))
-            value = product(split(value), (x_high[f], x_low[f]))
-            value = product(split(value), (own_high[f], own_low[f]))
-            image[f] = value
-        for f in range(0, FACES, 2):
-            one, two = split(image[f]), split(image[f + 1])
+    def own_parts(a):
+        return high[block(mine[a]), block(mine[a])], low[block(mine[a]), block(mine[a])]
+
+    def other_parts(a):
+        return other_high[a], other_low[a]
+
+    def x_parts_of(a):
+        return x_high[a], x_low[a]
+
+    def refine(bases):
+        systems, images = [], []
+        for a in range(3):
+            one, two = bases[a]
+            both = jnp.concatenate(
+                [product(split(one), other_parts(a)), product(split(two), own_parts(a))], axis=0
+            )
+            both = product(split(both), x_parts_of(a))
+            one = split(product(split(both[:NCON]), own_parts(a)))
+            two = split(product(split(both[NCON:]), other_parts(a)))
             gram = product(
                 one, [jnp.concatenate([blank, part, blank, blank], axis=0) for part in one], NT
             )
@@ -200,48 +249,67 @@
             )
             gram = gram + identity
             systems.append([gram[8 * v : 8 * v + 8] for v in range(4)])
+            images.append([jnp.concatenate([p, blank, q, blank], axis=0) for p, q in zip(one, two)])
         eliminate(systems, column_of, 4, False)
-        for f in range(0, FACES, 2):
-            factor = jnp.concatenate(systems[f // 2], axis=0)
+        new = []
+        for a in range(3):
+            factor = jnp.concatenate(systems[a], axis=0)
             factor = jnp.concatenate([factor * left_lanes, factor * right_lanes], axis=0)
-            one, two = split(image[f]), split(image[f + 1])
-            both = product(
-                split(factor),
-                [jnp.concatenate([p, blank, q, blank], axis=0) for p, q in zip(one, two)],
+            both = product(split(factor), images[a])
+            new.append((both[:NCON], both[NCON:]))
+        return new
+
+    bases = [(start[mine[a]], other_start[a]) for a in range(3)]
+    for _ in range(SUB_ITERS):
+        bases = refine(bases)
+    returns = []
+    for a in range(3):
+        basis[mine[a]] = bases[a][0]
+        basis[FACES + a] = bases[a][1]
+        returns.append(copy(5 * a + 3, basis.at[FACES + a], basis.at[theirs[a]], behind[a]))
+
+    def project(f, parts, columns):
+        for g in columns:
+            lower[block(f, NCON), block(g)] = product(
+                parts, (high[block(f), block(g)], low[block(f), block(g)])
             )
-            basis_out[f] = both[:NCON]
-            basis_out[f + 1] = both[NCON:]
-        return carry
-
-    lax.fori_loop(0, SUB_ITERS, iterate, 0)
-
-    wide[...] = jnp.zeros_like(wide)
-    for f in range(FACES):
-        wide[f * NCON : (f + 1) * NCON, f * FACE : (f + 1) * FACE] = basis_out[f]
-
-    lower[...] = jnp.zeros_like(lower)
-    for f in range(FACES):
-        parts = split(basis_out[f])
-        block = slice(f * FACE, (f + 1) * FACE)
-        out = slice(f * NCON, (f + 1) * NCON)
-        for g in range(f):
-            lower[out, g * FACE : (g + 1) * FACE] = product(
-                parts, split(schur[block, g * FACE : (g + 1) * FACE])
-            )
-        side = product(parts, (own_high[f], own_low[f]))
-        lower[out, block] = side
-        item[1, out, :] = product(parts, split(resid[block, :]))
-        side_out[f] = product(split(side), (x_high[f], x_low[f]))
+        wide[block(f, NCON), block(f)] = basis[f]
+        item[1, block(f, NCON), :] = product(parts, split(resid[block(f), :]))
+
+    mix_copies = []
+    for a in range(3):
+        f = mine[a]
+        parts = split(bases[a][0])
+        side = product(parts, own_parts(a))
+        lower[block(f, NCON), block(f)] = side
+        facing = product(split(bases[a][1]), other_parts(a))
+        both = product(split(jnp.concatenate([side, facing], axis=0)), x_parts_of(a))
+        mixes[f] = both
+        mixes[FACES + a] = jnp.concatenate([both[NCON:], both[:NCON]], axis=0)
+        mix_copies.append(copy(5 * a + 4, mixes.at[FACES + a], mixes.at[theirs[a]], behind[a]))
+        project(f, parts, mine[:a] + theirs)
+    for a in range(3):
+        returns[a].wait_recv()
+        f = theirs[a]
+        project(f, split(basis[f]), theirs[: a + 1])
     coarse = product(split(lower[...]), split(wide[...]), NT)
+    blocks_row = lax.broadcasted_iota(jnp.int32, (COARSE, COARSE), 0) // NCON
+    blocks_col = lax.broadcasted_iota(jnp.int32, (COARSE, COARSE), 1) // NCON
+    coarse = coarse + jnp.where(blocks_row == blocks_col, 0.0, coarse).T
     item[0, 0:64, 0:64] = coarse[0:64, 0:64]
     item[0, 0:64, 64:128] = coarse[128:192, 128:192]
     item[0, 64:192, :] = coarse[64:192, 0:128]
+    for a in range(3):
+        for c in faces[a]:
+            c.wait_send()
+        returns[a].wait_send()
+        mix_copies[a].wait()
 
 
 def back_kernel(
-    group_of, item, basis, partner, inverse, side, answer, mixed, partner_answer,
-    held, partial, relayed, arrived, passed, total, partner_basis, system,
-    send_sem, recv_sem, basis_send, basis_recv, answer_send, answer_recv,
+    group_of, item, mixes, answer, mixed, partner_answer,
+    held, partial, relayed, arrived, passed, total, system,
+    send_sem, recv_sem, answer_send, answer_recv,
 ):
     gx, gy, gz = here()
     x, core = gy // 2, lax.rem(gy, 2)
@@ -304,14 +372,6 @@
     mate_over = copy(slot(0, 0, 1), slot(0, 1, 1), over)
     pending.append(mate_over)
     spread(slot(0, 0, 1), 0, 1)
-    basis_copies = []
-    for f in range(FACES):
-        c = send(
-            basis.at[f], partner_basis.at[f ^ 1], basis_send.at[f], basis_recv.at[f ^ 1], across(f)
-        )
-        c.start()
-        basis_copies.append(c)
-
     held[0] = item[kind]
     held[16] = jnp.zeros((COARSE, COLS), F32)
 
@@ -387,38 +447,25 @@
     for up, down in first.values():
         up.wait_send()
         down.wait_send()
-    for c in basis_copies:
-        c.wait()
-
-    def mix(f, carry):
-        value = product(split(partner_basis[f]), split(partner[f]))
-        value = product(split(value), split(inverse[f]))
-        mixed[f] = jnp.concatenate([side[f], value], axis=0).T
-        return carry
-
-    lax.fori_loop(0, FACES, mix, 0)
+
+    for f in range(FACES):
+        mixed[f] = mixes[f].T
     last.wait()
 
     system[:, 0:COLS] = total[1]
     packed = total[0]
-    row64 = lax.broadcasted_iota(jnp.int32, (64, 64), 0) // NCON
-    col64 = lax.broadcasted_iota(jnp.int32, (64, 64), 1) // NCON
-
-    def fill(block):
-        return block + jnp.where(row64 > col64, block, 0.0).T
-
     one = packed[0:64, 0:64]
     below = packed[64:192, 0:64]
     middle = packed[64:128, 64:128]
     final = packed[128:192, 64:128]
     corner = packed[0:64, 64:128]
     blank = jnp.zeros((64, 64), F32)
-    system[0:64, COLS : COLS + 256] = jnp.concatenate([fill(one), below.T, blank], axis=1)
+    system[0:64, COLS : COLS + 256] = jnp.concatenate([one, below.T, blank], axis=1)
     system[64:192, COLS : COLS + 256] = jnp.concatenate(
         [
             below,
-            jnp.concatenate([fill(middle), final], axis=0),
-            jnp.concatenate([final.T, fill(corner)], axis=0),
+            jnp.concatenate([middle, final], axis=0),
+            jnp.concatenate([final.T, corner], axis=0),
             jnp.zeros((128, 64), F32),
         ],
         axis=1,
@@ -501,36 +548,34 @@
 
 def per_device(schur, start_block, resid, group_of):
     matrix = schur[0, 0, 0]
-    partner = pl.pallas_call(
-        faces_kernel,
-        out_shape=array(FACES, FACE, FACE),
-        in_specs=[ANY],
-        out_specs=ANY,
-        scratch_shapes=[DMA((FACES,)), DMA((FACES,))],
-        compiler_params=remote(0),
-        name="faces",
-    )(matrix)
-    blocks = (FACES, FACE, FACE)
-    item, basis, inverse, side = pl.pallas_call(
-        local_kernel,
-        out_shape=(
-            array(2, COARSE, COLS),
-            array(FACES, NCON, FACE),
-            array(*blocks),
-            array(FACES, NCON, FACE),
-        ),
-        in_specs=[ANY, VMEM, VMEM, VMEM],
-        out_specs=(VMEM,) * 4,
-        scratch_shapes=[pltpu.VMEM((ORDER, ORDER), F32)]
-        + [pltpu.VMEM(blocks, BF16)] * 6
-        + [
+    pairs = (3, FACE, FACE)
+    item, mixes = pl.pallas_call(
+        front_kernel,
+        out_shape=(array(2, COARSE, COLS), array(FACES + 3, 2 * NCON, FACE)),
+        in_specs=[ANY] * 3,
+        out_specs=(VMEM,) * 2,
+        scratch_shapes=[
+            pltpu.VMEM((ORDER, ORDER), F32),
+            pltpu.VMEM((ORDER, ORDER), BF16),
+            pltpu.VMEM((ORDER, ORDER), BF16),
+            pltpu.VMEM(pairs, F32),
+            pltpu.VMEM(pairs, BF16),
+            pltpu.VMEM(pairs, BF16),
+            pltpu.VMEM(pairs, BF16),
+            pltpu.VMEM(pairs, BF16),
             pltpu.VMEM((FACES, NCON, FACE), F32),
+            pltpu.VMEM((3, NCON, FACE), F32),
+            pltpu.VMEM((ORDER, COLS), F32),
+            pltpu.VMEM((FACES + 3, NCON, FACE), F32),
             pltpu.VMEM((COARSE, ORDER), F32),
             pltpu.VMEM((COARSE, ORDER), F32),
-            DMA((FACES,)),
+            DMA((15,)),
+            DMA((15,)),
+            DMA((8,)),
         ],
-        name="local",
-    )(matrix, partner, jnp.swapaxes(start_block[0, 0, 0], 1, 2), resid[0, 0, 0])
+        compiler_params=remote(0),
+        name="front",
+    )(matrix, jnp.swapaxes(start_block[0, 0, 0], 1, 2), resid[0, 0, 0])
     answer, mixed, partner_answer = pl.pallas_call(
         back_kernel,
         out_shape=(
@@ -538,7 +583,7 @@
             array(FACES, FACE, 2 * NCON),
             array(FACES, NCON, COLS),
         ),
-        in_specs=[SMEM] + [VMEM] * 5,
+        in_specs=[SMEM] + [VMEM] * 2,
         out_specs=(VMEM,) * 3,
         scratch_shapes=[
             pltpu.VMEM((17, COARSE, COLS), F32),
@@ -547,15 +592,14 @@
             pltpu.VMEM((2, 2, COARSE, COLS), F32),
             pltpu.VMEM((COARSE, COLS), F32),
             pltpu.VMEM((2, COARSE, COLS), F32),
-            pltpu.VMEM((FACES, NCON, FACE), F32),
             pltpu.VMEM((COARSE, 384), F32),
             DMA((26,)),
             DMA((26,)),
         ]
-        + [DMA((FACES,))] * 4,
+        + [DMA((FACES,))] * 2,
         compiler_params=remote(1),
         name="back",
-    )(group_of, item, basis, partner, inverse, side)
+    )(group_of, item, mixes)
     correction = pl.pallas_call(
         final_kernel,
         out_shape=array(ORDER, COLS),

time: 101 us -> 78.3 us (0.78)
  Pallas kernels: 99.9 us -> 78.2 us
    pallas_call x2 -> x1, Pallas kernels: 55 us -> 34.3 us  [per_device(): pl.pallas_call(front_kernel, out_shape=(array(2, COARSE, COLS), array(FAC...]
    pallas_call x1, Pallas kernels: 42.4 us -> 41.4 us  [per_device(): pl.pallas_call(back_kernel, out_shape=(array(FACES, NCON, COLS), array(FA...]
where the time goes in v3:
time: 78.3 us; the launch traced here: 78.2 us
  Pallas kernels  78.2 us (100%)
    pallas_call x1, Pallas kernels, per_device(): pl.pallas_call(back_kernel, out_shape=(array(FACES, NCON, COLS), array(FA...  41.4 us
    pallas_call x1, Pallas kernels, per_device(): pl.pallas_call(front_kernel, out_shape=(array(2, COARSE, COLS), array(FAC...  34.3 us
    pallas_call x1, Pallas kernels, per_device(): pl.pallas_call(final_kernel, out_shape=array(ORDER, COLS), in_specs=[VMEM...  2.53 us

profile of v3, /device:TPU:1, one launch (start us, length us, event | category | flops | bytes accessed | tf_op | source)
XLA Modules:
  0.0 78.2 jit_solution(3517761776688464023)
XLA Ops:
  0.0 34.3 %front.1 = (f32[2,192,128]{2,1,0:T(8,128)}, f32[9,64,256]{2,1,0:T(8,128)}) custom-call(f32[1536,1536]{1,0:T(8,128)} %bitcast.6, f32[6,32,256]{2,1,0:T(8,128)} %bitcast.8, f32[1536,128]{1,0:T(8,128)} %bitcast.7), custom_call_target="tpu_custom_call" | custom-call | tf_op jit(solution)/shard_map/front/pallas_call | solution.py:552
  34.3 41.4 %back.1 = (f32[6,32,128]{2,1,0:T(8,128)}, f32[6,256,64]{2,1,0:T(8,128)}, f32[6,32,128]{2,1,0:T(8,128)}) custom-call(s32[64]{0:T(128)} %group_of.1, f32[2,192,128]{2,1,0:T(8,128)} %get-tuple-element.10.item, f32[9,64,256]{2,1,0:T(8,128)} %get-tuple-element.11.mixes), custom_call_target="tpu_custom_call" | custom-call | tf_op jit(solution)/shard_map/back/pallas_call | solution.py:579
  75.7 2.5 %final.1 = f32[1536,128]{1,0:T(8,128)} custom-call(f32[6,256,64]{2,1,0:T(8,128)} %get-tuple-element.12.mixed, f32[6,32,128]{2,1,0:T(8,128)} %get-tuple-element.13.answer, f32[6,32,128]{2,1,0:T(8,128)} %get-tuple-element.14.partner_answer), custom_call_target="tpu_custom_call" | custom-call | tf_op jit(solution)/shard_map/final/pallas_call | solution.py:603

commit v4 on v3

--- a/solution.py
+++ b/solution.py
@@ -37,13 +37,6 @@
     if face < 4:
         return gx, lax.rem(gy + step + GY, GY), gz
     return gx, gy, lax.rem(gz + step + GZ, GZ)
-
-
-def greet(devices):
-    barrier = pltpu.get_barrier_semaphore()
-    for device in devices:
-        pl.semaphore_signal(barrier, inc=1, device_id=device, device_id_type=MESH)
-    pl.semaphore_wait(barrier, len(devices))
 
 
 def send(src, dst, send_sem, recv_sem, device):
@@ -112,10 +105,12 @@
                         columns[c][v] = updated
 
 
-def front_kernel(
-    schur_hbm, start_hbm, resid_hbm, item, mixes,
-    schur, high, low, other, other_high, other_low, x_high, x_low, start, other_start, resid,
-    basis, lower, wide, send_sem, recv_sem, load_sem,
+def main_kernel(
+    group_of, schur_hbm, start_hbm, resid_hbm, correction,
+    stage, packed_out, packed_in, schur, high, low, other, other_high, other_low, x_high, x_low, start, other_start, resid,
+    basis, lower, wide, item, mixes, mixed_high, mixed_low,
+    pieces, held, sums, got, total, system, answer, partner_answer,
+    send_sem, recv_sem, load_sem,
 ):
     gx, gy, gz = here()
     core = lax.rem(gy, 2)
@@ -132,6 +127,17 @@
 
     ahead = [along(a, 1 - 2 * turns[a]) for a in range(3)]
     behind = [along(a, 2 * turns[a] - 1) for a in range(3)]
+    x = gy // 2
+    y, z = gz // 2, lax.rem(gz, 2)
+
+    def plane_device(i, cc):
+        to_x, to_y, to_z = lax.rem(x + i % 4, 4), lax.rem(y + (i // 4) % 4, 4), lax.rem(z + i // 16, 2)
+        to_core = core + cc * (1 - 2 * core)
+        return to_core, (to_x * 4 + to_y) * 2 + to_z, (gx, 2 * to_x + to_core, 2 * to_y + to_z)
+
+    chip = (x * 4 + y) * 2 + z
+    line = gy * GZ + gz
+    plane = [plane_device(i, cc) for i in range(32) for cc in range(2) if i or cc]
 
     def block(f, size=FACE):
         return pl.ds(pl.multiple_of(f * size, size), size)
@@ -143,36 +149,44 @@
         copy.start()
         loads.append(copy)
 
+    for a in range(3):
+        load(schur_hbm.at[block(theirs[a]), block(theirs[a])], stage.at[a])
+    barrier = pltpu.get_barrier_semaphore()
+    greeted = [ahead[0], behind[0]] + [place for _, _, place in plane]
+    for device in greeted:
+        pl.semaphore_signal(barrier, inc=1, device_id=device, device_id_type=MESH)
     for f in range(FACES):
         rows = pl.ds(f * FACE, FACE)
         load(schur_hbm.at[rows, :], schur.at[rows, :])
     load(start_hbm, start)
     load(resid_hbm, resid)
-    greet(ahead + behind)
-
-    def copy(n, src, dst, device):
+    half = FACE // 2
+    half_rows = lax.broadcasted_iota(jnp.int32, (half, half), 0)
+    half_cols = lax.broadcasted_iota(jnp.int32, (half, half), 1)
+    for a in range(3):
+        loads[a].wait()
+        first_block = stage[a, 0:half, 0:half]
+        second_block = stage[a, half:FACE, half:FACE]
+        packed_out[a, 0:half] = stage[a, half:FACE, 0:half]
+        packed_out[a, half:FACE] = jnp.where(half_rows >= half_cols, first_block, second_block)
+        packed_out[a, FACE : FACE + 8] = jnp.broadcast_to(
+            jnp.sum(
+                jnp.where(half_rows == half_cols, second_block, 0.0), axis=0, keepdims=True
+            ),
+            (8, half),
+        )
+    pl.semaphore_wait(barrier, len(greeted))
+    counter = [0]
+
+    def copy(src, dst, device):
+        n = counter[0]
+        counter[0] += 1
         started = send(src, dst, send_sem.at[n], recv_sem.at[n], device)
         started.start()
         return started
 
-    half = FACE // 2
-    faces = {}
-    for a in (0, 2, 1):
-        f = theirs[a]
-        corner = pl.ds(pl.multiple_of(f * FACE, FACE), half)
-        bottom = pl.ds(pl.multiple_of(f * FACE + half, half), half)
-        faces[a] = [
-            copy(
-                5 * a, schur_hbm.at[bottom, block(f)], other.at[a, pl.ds(half, half), :], ahead[a]
-            ),
-            copy(
-                5 * a + 1,
-                schur_hbm.at[corner, corner],
-                other.at[a, pl.ds(0, half), pl.ds(0, half)],
-                ahead[a],
-            ),
-            copy(5 * a + 2, start_hbm.at[f], other_start.at[a], ahead[a]),
-        ]
+    faces = {a: copy(packed_out.at[a], packed_in.at[a], ahead[a]) for a in (2, 0, 1)}
+    starts = [copy(start_hbm.at[theirs[a]], other_start.at[a], ahead[a]) for a in range(3)]
 
     def divide(r, carry):
         rows = pl.ds(pl.multiple_of(r * 64, 64), 64)
@@ -182,18 +196,28 @@
     lower[...] = jnp.zeros_like(lower)
     wide[...] = jnp.zeros_like(wide)
     for f in range(FACES):
-        loads[f].wait()
+        loads[3 + f].wait()
         lax.fori_loop(f * 4, f * 4 + 4, divide, 0)
-    loads[6].wait()
-    loads[7].wait()
+    loads[9].wait()
+    loads[10].wait()
 
     row_ids = lax.broadcasted_iota(jnp.int32, (FACE, FACE), 0)
     col_ids = lax.broadcasted_iota(jnp.int32, (FACE, FACE), 1)
 
     def invert(a):
-        for c in faces[a]:
-            c.wait_recv()
-        other[a, 0:half, half:FACE] = other[a, half:FACE, 0:half].T
+        faces[a].wait_recv()
+        below = packed_in[a, 0:half]
+        folded = packed_in[a, half:FACE]
+        mirrored = folded.T
+        second_diagonal = jnp.broadcast_to(packed_in[a, FACE : FACE + 1], (half, half))
+        other[a, half:FACE, 0:half] = below
+        other[a, 0:half, half:FACE] = below.T
+        other[a, 0:half, 0:half] = jnp.where(half_rows >= half_cols, folded, mirrored)
+        other[a, half:FACE, half:FACE] = jnp.where(
+            half_rows < half_cols,
+            folded,
+            jnp.where(half_rows == half_cols, second_diagonal, mirrored),
+        )
         theirs_block = other[a]
         other_high[a], other_low[a] = split(theirs_block)
         total = schur[block(mine[a]), block(mine[a])] + theirs_block
@@ -259,6 +283,8 @@
             new.append((both[:NCON], both[NCON:]))
         return new
 
+    for c in starts:
+        c.wait_recv()
     bases = [(start[mine[a]], other_start[a]) for a in range(3)]
     for _ in range(SUB_ITERS):
         bases = refine(bases)
@@ -266,7 +292,7 @@
     for a in range(3):
         basis[mine[a]] = bases[a][0]
         basis[FACES + a] = bases[a][1]
-        returns.append(copy(5 * a + 3, basis.at[FACES + a], basis.at[theirs[a]], behind[a]))
+        returns.append(copy(basis.at[FACES + a], basis.at[theirs[a]], behind[a]))
 
     def project(f, parts, columns):
         for g in columns:
@@ -286,7 +312,7 @@
         both = product(split(jnp.concatenate([side, facing], axis=0)), x_parts_of(a))
         mixes[f] = both
         mixes[FACES + a] = jnp.concatenate([both[NCON:], both[:NCON]], axis=0)
-        mix_copies.append(copy(5 * a + 4, mixes.at[FACES + a], mixes.at[theirs[a]], behind[a]))
+        mix_copies.append(copy(mixes.at[FACES + a], mixes.at[theirs[a]], behind[a]))
         project(f, parts, mine[:a] + theirs)
     for a in range(3):
         returns[a].wait_recv()
@@ -299,158 +325,47 @@
     item[0, 0:64, 0:64] = coarse[0:64, 0:64]
     item[0, 0:64, 64:128] = coarse[128:192, 128:192]
     item[0, 64:192, :] = coarse[64:192, 0:128]
-    for a in range(3):
-        for c in faces[a]:
-            c.wait_send()
-        returns[a].wait_send()
-        mix_copies[a].wait()
-
-
-def back_kernel(
-    group_of, item, mixes, answer, mixed, partner_answer,
-    held, partial, relayed, arrived, passed, total, system,
-    send_sem, recv_sem, answer_send, answer_recv,
-):
-    gx, gy, gz = here()
-    x, core = gy // 2, lax.rem(gy, 2)
-    y, z = gz // 2, lax.rem(gz, 2)
-    kind = core
-
-    def ring(step):
-        nx = lax.rem(x + (1 - core) * step, 4)
-        ny = lax.rem(y + core * step, 4)
-        return gx, 2 * nx + core, 2 * ny + z
-
-    def other_ring(step):
-        nx = lax.rem(x + core * step, 4)
-        ny = lax.rem(y + (1 - core) * step, 4)
-        return gx, 2 * nx + core, 2 * ny + z
-
-    mate = (gx, 2 * x + (1 - core), gz)
-    over = (gx, gy, 2 * y + (1 - z))
-    targets = [mate, over] + [ring(s) for s in (1, 3)] + [other_ring(s) for s in (1, 3)]
-    greet(targets + [across(f) for f in range(FACES)])
-
-    half = COARSE // 2
-    counter = [0]
-
-    def copy(src, dst, device):
-        n = counter[0]
-        counter[0] += 1
-        started = send(src, dst, send_sem.at[n], recv_sem.at[n], device)
-        started.start()
-        return started
-
-    def slot(step, zz, cc):
-        return held.at[4 * step + 2 * zz + cc]
-
-    swap = copy(item.at[1 - kind], slot(0, 0, 1), mate)
-    own_over = copy(item.at[kind], slot(0, 1, 0), over)
-    pending = [swap, own_over]
-    first = {}
-
-    def spread(src, zz, cc):
-        first[zz, cc] = (
-            copy(src, slot(1, zz, cc), ring(1)),
-            copy(src, slot(3, zz, cc), ring(3)),
-        )
-
-    def relay(zz, cc):
-        up, down = first[zz, cc]
-        top, bottom = pl.ds(0, half), pl.ds(half, half)
-        up.wait_recv()
-        pending.append(
-            copy(slot(1, zz, cc).at[top, :], slot(2, zz, cc).at[top, :], ring(1))
-        )
-        down.wait_recv()
-        pending.append(
-            copy(slot(3, zz, cc).at[bottom, :], slot(2, zz, cc).at[bottom, :], ring(3))
-        )
-
-    spread(item.at[kind], 0, 0)
-    swap.wait_recv()
-    mate_over = copy(slot(0, 0, 1), slot(0, 1, 1), over)
-    pending.append(mate_over)
-    spread(slot(0, 0, 1), 0, 1)
-    held[0] = item[kind]
-    held[16] = jnp.zeros((COARSE, COLS), F32)
-
-    def group_at(place, cc, flip=0):
-        _, gy_at, gz_at = place
-        gy_at = gy_at + cc * (1 - 2 * core)
-        gz_at = gz_at + flip * (1 - 2 * z)
-        return group_of[gy_at * GZ + gz_at]
-
-    source_groups = [
-        group_at(ring((4 - s // 4) % 4), s % 2, (s // 2) % 2) for s in range(16)
+
+    def six(ref, index):
+        return ref.at[pl.ds(pl.multiple_of(index * 8, 8), 6), :]
+
+    for k in range(2):
+        for c in range(32):
+            pieces[8 * (32 * k + c) : 8 * (32 * k + c) + 6, :] = item[k, 6 * c : 6 * c + 6, :]
+    scattered = [
+        copy(six(pieces, 32 * to_core + to_chip), six(held, line), place)
+        for to_core, to_chip, place in plane
     ]
-    members = {}
-    for step in range(4):
-        for cc in (0, 1):
-            goal = group_at(other_ring(step), cc)
-            slots = [jnp.int32(16)] * 4
-            for s in range(16):
-                hit = source_groups[s] == goal
-                slots = [
-                    jnp.where(hit, new, old)
-                    for new, old in zip([jnp.int32(s)] + slots[:3], slots)
-                ]
-            members[step, cc] = slots
-
-    own_over.wait_recv()
-    spread(slot(0, 1, 0), 1, 0)
-    mate_over.wait_recv()
-    spread(slot(0, 1, 1), 1, 1)
-    relay(0, 0)
-    relay(0, 1)
-    relay(1, 0)
-    relay(1, 1)
-    for c in pending[3:]:
+    here_six = pl.ds(pl.multiple_of(line * 8, 8), 6)
+    held[here_six, :] = pieces[pl.ds(pl.multiple_of((32 * core + chip) * 8, 8), 6), :]
+    groups = jnp.broadcast_to(group_of[...].astype(F32), (64, 64))
+    same = jnp.where(groups == groups.T, 1.0, 0.0).astype(BF16)
+    for a in range(3):
+        mix_copies[a].wait_recv()
+    for f in range(FACES):
+        mixed_high[f], mixed_low[f] = split(mixes[f].T)
+    for c in scattered:
         c.wait_recv()
-
-    def gather_members(step):
-        for cc in (0, 1):
-            slots = members[step, cc]
-
-            def add_rows(r, carry):
-                block = pl.ds(pl.multiple_of(r * 32, 32), 32)
-                low = held[slots[0], block, :] + held[slots[1], block, :]
-                high = held[slots[2], block, :] + held[slots[3], block, :]
-                partial[step, cc, block, :] = low + high
-                return carry
-
-            lax.fori_loop(0, COARSE // 32, add_rows, 0)
-
-    top, bottom = pl.ds(0, half), pl.ds(half, half)
-    gather_members(2)
-    relay_up = copy(partial.at[2, :, top, :], relayed.at[0], other_ring(1))
-    relay_down = copy(partial.at[2, :, bottom, :], relayed.at[1], other_ring(3))
-    gather_members(1)
-    up_two = copy(partial.at[1, :, bottom, :], arrived.at[0, :, bottom, :], other_ring(1))
-    gather_members(3)
-    down_two = copy(partial.at[3, :, top, :], arrived.at[1, :, top, :], other_ring(3))
-    relay_up.wait_recv()
-    partial[1, :, top, :] = partial[1, :, top, :] + relayed[0]
-    up_one = copy(partial.at[1, :, top, :], arrived.at[0, :, top, :], other_ring(1))
-    relay_down.wait_recv()
-    partial[3, :, bottom, :] = partial[3, :, bottom, :] + relayed[1]
-    down_one = copy(partial.at[3, :, bottom, :], arrived.at[1, :, bottom, :], other_ring(3))
-    gather_members(0)
-    sends = [relay_up, relay_down, up_two, down_two, up_one, down_one]
-    for c in sends[2:]:
+    for j in range(6):
+        value = held[pl.ds(j, 64, stride=8), :]
+        one = value.astype(BF16)
+        rest = value - one.astype(F32)
+        two = rest.astype(BF16)
+        three = (rest - two.astype(F32)).astype(BF16)
+        added = lax.dot_general(
+            same, jnp.concatenate([one, two, three], axis=1), NN, preferred_element_type=F32
+        )
+        sums[pl.ds(j, 64, stride=8), :] = added[:, 0:128] + (added[:, 128:256] + added[:, 256:384])
+    returned = [
+        copy(six(sums, place[1] * GZ + place[2]), six(got, 32 * core + chip), place)
+        for _, _, place in plane
+    ]
+    got[pl.ds(pl.multiple_of((32 * core + chip) * 8, 8), 6), :] = sums[here_six, :]
+    for c in returned:
         c.wait_recv()
-    passed[...] = partial[0, 1] + arrived[0, 1] + arrived[1, 1]
-    last = copy(passed, total.at[kind], mate)
-    total[kind] = partial[0, 0] + arrived[0, 0] + arrived[1, 0]
-    for c in pending + sends:
-        c.wait_send()
-    for up, down in first.values():
-        up.wait_send()
-        down.wait_send()
-
-    for f in range(FACES):
-        mixed[f] = mixes[f].T
-    last.wait()
+    for k in range(2):
+        for c in range(32):
+            total[k, 6 * c : 6 * c + 6, :] = got[8 * (32 * k + c) : 8 * (32 * k + c) + 6, :]
 
     system[:, 0:COLS] = total[1]
     packed = total[0]
@@ -517,22 +432,20 @@
         system[...] = system[...] - update
         system[rows, :] = scaled
     answer[...] = system[:, 0:COLS].reshape(FACES, NCON, COLS)
-    copies = []
-    for f in range(FACES):
-        c = send(
-            answer.at[f], partner_answer.at[f ^ 1], answer_send.at[f], answer_recv.at[f ^ 1],
-            across(f),
-        )
-        c.start()
-        copies.append(c)
-    for c in copies:
-        c.wait()
-
-
-def final_kernel(mixed, answer, partner_answer, correction):
-    for f in range(FACES):
+    answers = [
+        copy(answer.at[f], partner_answer.at[f ^ 1], across(f)) for f in range(FACES)
+    ]
+    for f in (2, 3, 4, 5, 0, 1):
+        answers[f ^ 1].wait_recv()
         both = jnp.concatenate([answer[f], partner_answer[f]], axis=0)
-        correction[f * FACE : (f + 1) * FACE, :] = product(split(mixed[f]), split(both))
+        correction[f * FACE : (f + 1) * FACE, :] = product(
+            (mixed_high[f], mixed_low[f]), split(both)
+        )
+    for a in range(3):
+        for c in (faces[a], starts[a], returns[a], mix_copies[a]):
+            c.wait_send()
+    for c in scattered + returned + answers:
+        c.wait_send()
 
 
 def array(*shape):
@@ -549,12 +462,16 @@
 def per_device(schur, start_block, resid, group_of):
     matrix = schur[0, 0, 0]
     pairs = (3, FACE, FACE)
-    item, mixes = pl.pallas_call(
-        front_kernel,
-        out_shape=(array(2, COARSE, COLS), array(FACES + 3, 2 * NCON, FACE)),
-        in_specs=[ANY] * 3,
-        out_specs=(VMEM,) * 2,
+    copies = 12 + 2 * 63 + 6
+    correction = pl.pallas_call(
+        main_kernel,
+        out_shape=array(ORDER, COLS),
+        in_specs=[VMEM] + [ANY] * 3,
+        out_specs=VMEM,
         scratch_shapes=[
+            pltpu.VMEM(pairs, F32),
+            pltpu.VMEM((3, FACE + 8, FACE // 2), F32),
+            pltpu.VMEM((3, FACE + 8, FACE // 2), F32),
             pltpu.VMEM((ORDER, ORDER), F32),
             pltpu.VMEM((ORDER, ORDER), BF16),
             pltpu.VMEM((ORDER, ORDER), BF16),
@@ -569,44 +486,25 @@
             pltpu.VMEM((FACES + 3, NCON, FACE), F32),
             pltpu.VMEM((COARSE, ORDER), F32),
             pltpu.VMEM((COARSE, ORDER), F32),
-            DMA((15,)),
-            DMA((15,)),
-            DMA((8,)),
+            pltpu.VMEM((2, COARSE, COLS), F32),
+            pltpu.VMEM((FACES + 3, 2 * NCON, FACE), F32),
+            pltpu.VMEM((FACES, FACE, 2 * NCON), BF16),
+            pltpu.VMEM((FACES, FACE, 2 * NCON), BF16),
+            pltpu.VMEM((512, COLS), F32),
+            pltpu.VMEM((512, COLS), F32),
+            pltpu.VMEM((512, COLS), F32),
+            pltpu.VMEM((512, COLS), F32),
+            pltpu.VMEM((2, COARSE, COLS), F32),
+            pltpu.VMEM((COARSE, 384), F32),
+            pltpu.VMEM((FACES, NCON, COLS), F32),
+            pltpu.VMEM((FACES, NCON, COLS), F32),
+            DMA((copies,)),
+            DMA((copies,)),
+            DMA((11,)),
         ],
         compiler_params=remote(0),
-        name="front",
-    )(matrix, jnp.swapaxes(start_block[0, 0, 0], 1, 2), resid[0, 0, 0])
-    answer, mixed, partner_answer = pl.pallas_call(
-        back_kernel,
-        out_shape=(
-            array(FACES, NCON, COLS),
-            array(FACES, FACE, 2 * NCON),
-            array(FACES, NCON, COLS),
-        ),
-        in_specs=[SMEM] + [VMEM] * 2,
-        out_specs=(VMEM,) * 3,
-        scratch_shapes=[
-            pltpu.VMEM((17, COARSE, COLS), F32),
-            pltpu.VMEM((4, 2, COARSE, COLS), F32),
-            pltpu.VMEM((2, 2, COARSE // 2, COLS), F32),
-            pltpu.VMEM((2, 2, COARSE, COLS), F32),
-            pltpu.VMEM((COARSE, COLS), F32),
-            pltpu.VMEM((2, COARSE, COLS), F32),
-            pltpu.VMEM((COARSE, 384), F32),
-            DMA((26,)),
-            DMA((26,)),
-        ]
-        + [DMA((FACES,))] * 2,
-        compiler_params=remote(1),
-        name="back",
-    )(group_of, item, mixes)
-    correction = pl.pallas_call(
-        final_kernel,
-        out_shape=array(ORDER, COLS),
-        in_specs=[VMEM] * 3,
-        out_specs=VMEM,
-        name="final",
-    )(mixed, answer, partner_answer)
+        name="main",
+    )(group_of[None], matrix, jnp.swapaxes(start_block[0, 0, 0], 1, 2), resid[0, 0, 0])
     return correction[None, None, None]
 
 

time: 78.3 us -> 65.8 us (0.84)
  Pallas kernels: 78.2 us -> 63.6 us
  local copies, waits for them, and re-layouts: 0 us -> 2.06 us
    pallas_call x3 -> x1, Pallas kernels: 78.2 us -> 63.6 us  [per_device(): pl.pallas_call(main_kernel, out_shape=array(ORDER, COLS), in_specs=[VMEM]...]
    unnamed x0 -> x1, local copies, waits for them, and re-layouts: none -> 2.06 us
where the time goes in v4:
time: 65.8 us; the launch traced here: 65.7 us
  Pallas kernels  63.6 us (97%)
  local copies, waits for them, and re-layouts  2.06 us (3%)
    pallas_call x1, Pallas kernels, per_device(): pl.pallas_call(main_kernel, out_shape=array(ORDER, COLS), in_specs=[VMEM]...  63.6 us
    unnamed x1, local copies, waits for them, and re-layouts  2.06 us

profile of v4, /device:TPU:1, one launch (start us, length us, event | category | flops | bytes accessed | tf_op | source)
XLA Modules:
  0.0 65.7 jit_solution(2042658129136839946)
XLA Ops:
  0.0 63.6 %main.1 = f32[1536,128]{1,0:T(8,128)} custom-call(s32[1,64]{1,0:T(1,128)} %bitcast.11, f32[1536,1536]{1,0:T(8,128)} %bitcast.7, f32[6,32,256]{2,1,0:T(8,128)} %bitcast.10, f32[1536,128]{1,0:T(8,128)} %bitcast.9), custom_call_target="tpu_custom_call" | custom-call | tf_op jit(solution)/shard_map/main/pallas_call | solution.py:466
  63.6 2.1 %copy.6 = f32[1,1,1,1536,128]{4,3,2,1,0:T(8,128)} copy(f32[1,1,1,1536,128]{4,3,2,1,0:T(8,128)} %bitcast.8) | data formatting | bytes 1572864

commit v5 on v4

--- a/solution.py
+++ b/solution.py
@@ -110,7 +110,7 @@
     stage, packed_out, packed_in, schur, high, low, other, other_high, other_low, x_high, x_low, start, other_start, resid,
     basis, lower, wide, item, mixes, mixed_high, mixed_low,
     pieces, held, sums, got, total, system, answer, partner_answer,
-    send_sem, recv_sem, load_sem,
+    send_sem, recv_sem, load_sem, plane_sem,
 ):
     gx, gy, gz = here()
     core = lax.rem(gy, 2)
@@ -137,7 +137,9 @@
 
     chip = (x * 4 + y) * 2 + z
     line = gy * GZ + gz
-    plane = [plane_device(i, cc) for i in range(32) for cc in range(2) if i or cc]
+    hops = {i: (i % 4) * (4 - i % 4) + (i // 4 % 4) * (4 - i // 4 % 4) + 3 * (i // 16) for i in range(32)}
+    far_first = sorted(range(32), key=lambda i: -hops[i])
+    plane = [plane_device(i, cc) for i in far_first for cc in range(2) if i or cc]
 
     def block(f, size=FACE):
         return pl.ds(pl.multiple_of(f * size, size), size)
@@ -152,7 +154,9 @@
     for a in range(3):
         load(schur_hbm.at[block(theirs[a]), block(theirs[a])], stage.at[a])
     barrier = pltpu.get_barrier_semaphore()
-    greeted = [ahead[0], behind[0]] + [place for _, _, place in plane]
+    row_devices = [(gx, lax.rem(gy + i, GY), gz) for i in range(1, GY)]
+    column_devices = [(gx, gy, lax.rem(gz + i, GZ)) for i in range(1, GZ)]
+    greeted = [ahead[0], behind[0]] + row_devices + column_devices
     for device in greeted:
         pl.semaphore_signal(barrier, inc=1, device_id=device, device_id_type=MESH)
     for f in range(FACES):
@@ -176,6 +180,8 @@
             (8, half),
         )
     pl.semaphore_wait(barrier, len(greeted))
+    for device in row_devices:
+        pl.semaphore_signal(plane_sem, inc=1, device_id=device, device_id_type=MESH)
     counter = [0]
 
     def copy(src, dst, device):
@@ -329,6 +335,7 @@
     def six(ref, index):
         return ref.at[pl.ds(pl.multiple_of(index * 8, 8), 6), :]
 
+    pl.semaphore_wait(plane_sem, GY - 1)
     for k in range(2):
         for c in range(32):
             pieces[8 * (32 * k + c) : 8 * (32 * k + c) + 6, :] = item[k, 6 * c : 6 * c + 6, :]
@@ -414,23 +421,29 @@
             lambda slab, c, place=place: jnp.broadcast_to(
                 slab[:, place + c : place + c + 1], slab.shape
             ),
-            8,
+            16,
             True,
         )
         pivot_inverse = jnp.where(in_unit, jnp.concatenate(slabs, axis=0), 0.0)
         scaled = product(
             split(pivot_inverse), [placed(part, unit) for part in split(system[rows, :])]
         )
-        column = jnp.where(
-            (tall_lane >= place)
-            & (tall_lane < place + NCON)
-            & ((tall_row < k * NCON) | (tall_row >= (k + 1) * NCON)),
-            system[:, tile],
-            0.0,
-        )
-        update = product(split(column), [placed(part, place) for part in split(scaled)])
-        system[...] = system[...] - update
+        column = split(
+            jnp.where(
+                (tall_lane >= place) & (tall_lane < place + NCON), system[:, tile], 0.0
+            )
+        )
+        scaled_parts = [placed(part, place) for part in split(scaled)]
         system[rows, :] = scaled
+
+        def clear(low_row, high_row):
+            if low_row < high_row:
+                update = product([part[low_row:high_row] for part in column], scaled_parts)
+                system[low_row:high_row, :] = system[low_row:high_row, :] - update
+
+        clear((k + 1) * NCON, min((k + 2) * NCON, COARSE))
+        clear((k + 2) * NCON, COARSE)
+        clear(0, k * NCON)
     answer[...] = system[:, 0:COLS].reshape(FACES, NCON, COLS)
     answers = [
         copy(answer.at[f], partner_answer.at[f ^ 1], across(f)) for f in range(FACES)
@@ -501,6 +514,7 @@
             DMA((copies,)),
             DMA((copies,)),
             DMA((11,)),
+            pltpu.SemaphoreType.REGULAR,
         ],
         compiler_params=remote(0),
         name="main",

time: 65.8 us -> 60.6 us (0.921)
  Pallas kernels: 63.6 us -> 58.4 us
    pallas_call x1, Pallas kernels: 63.6 us -> 58.4 us  [per_device(): pl.pallas_call(main_kernel, out_shape=array(ORDER, COLS), in_specs=[VMEM]...]
where the time goes in v5:
time: 60.6 us; the launch traced here: 60.5 us
  Pallas kernels  58.4 us (96%)
  local copies, waits for them, and re-layouts  2.06 us (3%)
    pallas_call x1, Pallas kernels, per_device(): pl.pallas_call(main_kernel, out_shape=array(ORDER, COLS), in_specs=[VMEM]...  58.4 us
    unnamed x1, local copies, waits for them, and re-layouts  2.06 us

profile of v5, /device:TPU:1, one launch (start us, length us, event | category | flops | bytes accessed | tf_op | source)
XLA Modules:
  0.0 60.5 jit_solution(7801216604509907510)
XLA Ops:
  0.0 58.4 %main.1 = f32[1536,128]{1,0:T(8,128)} custom-call(s32[1,64]{1,0:T(1,128)} %bitcast.11, f32[1536,1536]{1,0:T(8,128)} %bitcast.7, f32[6,32,256]{2,1,0:T(8,128)} %bitcast.10, f32[1536,128]{1,0:T(8,128)} %bitcast.9), custom_call_target="tpu_custom_call" | custom-call | tf_op jit(solution)/shard_map/main/pallas_call | solution.py:479
  58.4 2.1 %copy.6 = f32[1,1,1,1536,128]{4,3,2,1,0:T(8,128)} copy(f32[1,1,1,1536,128]{4,3,2,1,0:T(8,128)} %bitcast.8) | data formatting | bytes 1572864

commit v6 on v5

--- a/solution.py
+++ b/solution.py
@@ -108,7 +108,7 @@
 def main_kernel(
     group_of, schur_hbm, start_hbm, resid_hbm, correction,
     stage, packed_out, packed_in, schur, high, low, other, other_high, other_low, x_high, x_low, start, other_start, resid,
-    basis, lower, wide, item, mixes, mixed_high, mixed_low,
+    basis, lower_high, lower_low, wide_high, wide_low, item, mixes, mixed_high, mixed_low,
     pieces, held, sums, got, total, system, answer, partner_answer,
     send_sem, recv_sem, load_sem, plane_sem,
 ):
@@ -199,8 +199,8 @@
         high[rows, :], low[rows, :] = split(schur[rows, :])
         return carry
 
-    lower[...] = jnp.zeros_like(lower)
-    wide[...] = jnp.zeros_like(wide)
+    for ref in (lower_high, lower_low, wide_high, wide_low):
+        ref[...] = jnp.zeros_like(ref)
     for f in range(FACES):
         loads[3 + f].wait()
         lax.fori_loop(f * 4, f * 4 + 4, divide, 0)
@@ -263,14 +263,25 @@
 
     def refine(bases):
         systems, images = [], []
-        for a in range(3):
-            one, two = bases[a]
-            both = jnp.concatenate(
-                [product(split(one), other_parts(a)), product(split(two), own_parts(a))], axis=0
+        values = [
+            jnp.concatenate(
+                [
+                    product(split(bases[a][0]), other_parts(a)),
+                    product(split(bases[a][1]), own_parts(a)),
+                ],
+                axis=0,
             )
-            both = product(split(both), x_parts_of(a))
-            one = split(product(split(both[:NCON]), own_parts(a)))
-            two = split(product(split(both[NCON:]), other_parts(a)))
+            for a in range(3)
+        ]
+        values = [product(split(values[a]), x_parts_of(a)) for a in range(3)]
+        values = [
+            (
+                split(product(split(values[a][:NCON]), own_parts(a))),
+                split(product(split(values[a][NCON:]), other_parts(a))),
+            )
+            for a in range(3)
+        ]
+        for one, two in values:
             gram = product(
                 one, [jnp.concatenate([blank, part, blank, blank], axis=0) for part in one], NT
             )
@@ -301,19 +312,20 @@
         returns.append(copy(basis.at[FACES + a], basis.at[theirs[a]], behind[a]))
 
     def project(f, parts, columns):
+        rows = block(f, NCON)
         for g in columns:
-            lower[block(f, NCON), block(g)] = product(
-                parts, (high[block(f), block(g)], low[block(f), block(g)])
+            lower_high[rows, block(g)], lower_low[rows, block(g)] = split(
+                product(parts, (high[block(f), block(g)], low[block(f), block(g)]))
             )
-        wide[block(f, NCON), block(f)] = basis[f]
-        item[1, block(f, NCON), :] = product(parts, split(resid[block(f), :]))
+        wide_high[rows, block(f)], wide_low[rows, block(f)] = parts
+        item[1, rows, :] = product(parts, split(resid[block(f), :]))
 
     mix_copies = []
     for a in range(3):
         f = mine[a]
         parts = split(bases[a][0])
         side = product(parts, own_parts(a))
-        lower[block(f, NCON), block(f)] = side
+        lower_high[block(f, NCON), block(f)], lower_low[block(f, NCON), block(f)] = split(side)
         facing = product(split(bases[a][1]), other_parts(a))
         both = product(split(jnp.concatenate([side, facing], axis=0)), x_parts_of(a))
         mixes[f] = both
@@ -324,7 +336,9 @@
         returns[a].wait_recv()
         f = theirs[a]
         project(f, split(basis[f]), theirs[: a + 1])
-    coarse = product(split(lower[...]), split(wide[...]), NT)
+    coarse = product(
+        (lower_high[...], lower_low[...]), (wide_high[...], wide_low[...]), NT
+    )
     blocks_row = lax.broadcasted_iota(jnp.int32, (COARSE, COARSE), 0) // NCON
     blocks_col = lax.broadcasted_iota(jnp.int32, (COARSE, COARSE), 1) // NCON
     coarse = coarse + jnp.where(blocks_row == blocks_col, 0.0, coarse).T
@@ -408,6 +422,7 @@
 
     for k in range(FACES):
         rows = slice(k * NCON, (k + 1) * NCON)
+        live = slice(0, COLS if k == FACES - 1 else 384)
         tile = slice(COLS + 128 * (k // 4), COLS + 128 * (k // 4) + 128)
         place = (k % 4) * NCON
         unit = (place + NCON) % 128
@@ -426,7 +441,7 @@
         )
         pivot_inverse = jnp.where(in_unit, jnp.concatenate(slabs, axis=0), 0.0)
         scaled = product(
-            split(pivot_inverse), [placed(part, unit) for part in split(system[rows, :])]
+            split(pivot_inverse), [placed(part, unit) for part in split(system[rows, live])]
         )
         column = split(
             jnp.where(
@@ -434,12 +449,12 @@
             )
         )
         scaled_parts = [placed(part, place) for part in split(scaled)]
-        system[rows, :] = scaled
+        system[rows, live] = scaled
 
         def clear(low_row, high_row):
             if low_row < high_row:
                 update = product([part[low_row:high_row] for part in column], scaled_parts)
-                system[low_row:high_row, :] = system[low_row:high_row, :] - update
+                system[low_row:high_row, live] = system[low_row:high_row, live] - update
 
         clear((k + 1) * NCON, min((k + 2) * NCON, COARSE))
         clear((k + 2) * NCON, COARSE)
@@ -497,8 +512,10 @@
             pltpu.VMEM((3, NCON, FACE), F32),
             pltpu.VMEM((ORDER, COLS), F32),
             pltpu.VMEM((FACES + 3, NCON, FACE), F32),
-            pltpu.VMEM((COARSE, ORDER), F32),
-            pltpu.VMEM((COARSE, ORDER), F32),
+            pltpu.VMEM((COARSE, ORDER), BF16),
+            pltpu.VMEM((COARSE, ORDER), BF16),
+            pltpu.VMEM((COARSE, ORDER), BF16),
+            pltpu.VMEM((COARSE, ORDER), BF16),
             pltpu.VMEM((2, COARSE, COLS), F32),
             pltpu.VMEM((FACES + 3, 2 * NCON, FACE), F32),
             pltpu.VMEM((FACES, FACE, 2 * NCON), BF16),

time: 60.6 us -> 58.7 us (0.969)
  Pallas kernels: 58.4 us -> 56.5 us
    pallas_call x1, Pallas kernels: 58.4 us -> 56.5 us  [per_device(): pl.pallas_call(main_kernel, out_shape=array(ORDER, COLS), in_specs=[VMEM]...]
where the time goes in v6:
time: 58.7 us; the launch traced here: 58.5 us
  Pallas kernels  56.5 us (96%)
  local copies, waits for them, and re-layouts  2.06 us (4%)
    pallas_call x1, Pallas kernels, per_device(): pl.pallas_call(main_kernel, out_shape=array(ORDER, COLS), in_specs=[VMEM]...  56.5 us
    unnamed x1, local copies, waits for them, and re-layouts  2.06 us

profile of v6, /device:TPU:1, one launch (start us, length us, event | category | flops | bytes accessed | tf_op | source)
XLA Modules:
  0.0 58.5 jit_solution(14162184170429739031)
XLA Ops:
  0.0 56.5 %main.1 = f32[1536,128]{1,0:T(8,128)} custom-call(s32[1,64]{1,0:T(1,128)} %bitcast.11, f32[1536,1536]{1,0:T(8,128)} %bitcast.7, f32[6,32,256]{2,1,0:T(8,128)} %bitcast.10, f32[1536,128]{1,0:T(8,128)} %bitcast.9), custom_call_target="tpu_custom_call" | custom-call | tf_op jit(solution)/shard_map/main/pallas_call | solution.py:494
  56.5 2.1 %copy.6 = f32[1,1,1,1536,128]{4,3,2,1,0:T(8,128)} copy(f32[1,1,1,1536,128]{4,3,2,1,0:T(8,128)} %bitcast.8) | data formatting | bytes 1572864

commit v7 on v6

--- a/solution.py
+++ b/solution.py
@@ -321,17 +321,22 @@
         item[1, rows, :] = product(parts, split(resid[block(f), :]))
 
     mix_copies = []
+    parts = [split(bases[a][0]) for a in range(3)]
+    sides = [product(parts[a], own_parts(a)) for a in range(3)]
+    facing = [product(split(bases[a][1]), other_parts(a)) for a in range(3)]
+    both = [
+        product(split(jnp.concatenate([sides[a], facing[a]], axis=0)), x_parts_of(a))
+        for a in range(3)
+    ]
     for a in range(3):
         f = mine[a]
-        parts = split(bases[a][0])
-        side = product(parts, own_parts(a))
-        lower_high[block(f, NCON), block(f)], lower_low[block(f, NCON), block(f)] = split(side)
-        facing = product(split(bases[a][1]), other_parts(a))
-        both = product(split(jnp.concatenate([side, facing], axis=0)), x_parts_of(a))
-        mixes[f] = both
-        mixes[FACES + a] = jnp.concatenate([both[NCON:], both[:NCON]], axis=0)
+        rows = block(f, NCON)
+        lower_high[rows, block(f)], lower_low[rows, block(f)] = split(sides[a])
+        mixes[f] = both[a]
+        mixes[FACES + a] = jnp.concatenate([both[a][NCON:], both[a][:NCON]], axis=0)
         mix_copies.append(copy(mixes.at[FACES + a], mixes.at[theirs[a]], behind[a]))
-        project(f, parts, mine[:a] + theirs)
+    for a in range(3):
+        project(mine[a], parts[a], mine[:a] + theirs)
     for a in range(3):
         returns[a].wait_recv()
         f = theirs[a]

time: 58.7 us -> 58.5 us (level)
  no operation moved by 1% of the time
where the time goes in v7:
time: 58.5 us; the launch traced here: 58.3 us
  Pallas kernels  56.3 us (96%)
  local copies, waits for them, and re-layouts  2.06 us (4%)
    pallas_call x1, Pallas kernels, per_device(): pl.pallas_call(main_kernel, out_shape=array(ORDER, COLS), in_specs=[VMEM]...  56.3 us
    unnamed x1, local copies, waits for them, and re-layouts  2.06 us

profile of v7, /device:TPU:1, one launch (start us, length us, event | category | flops | bytes accessed | tf_op | source)
XLA Modules:
  0.0 58.3 jit_solution(17890900054723647993)
XLA Ops:
  0.0 56.3 %main.1 = f32[1536,128]{1,0:T(8,128)} custom-call(s32[1,64]{1,0:T(1,128)} %bitcast.11, f32[1536,1536]{1,0:T(8,128)} %bitcast.7, f32[6,32,256]{2,1,0:T(8,128)} %bitcast.10, f32[1536,128]{1,0:T(8,128)} %bitcast.9), custom_call_target="tpu_custom_call" | custom-call | tf_op jit(solution)/shard_map/main/pallas_call | solution.py:499
  56.3 2.1 %copy.6 = f32[1,1,1,1536,128]{4,3,2,1,0:T(8,128)} copy(f32[1,1,1,1536,128]{4,3,2,1,0:T(8,128)} %bitcast.8) | data formatting | bytes 1572864
